TPU v7x, 256 devices: a whole 4x4x8 slice. The times are simulated.
256 devices in a mesh: rows: 4 (over z_hi, core), mp: 64 (over x, y, z_lo).
Axes of the slice: x: 4, y: 4, z: 8 (z_hi: 2, z_lo: 4; z = z_hi * 4 + z_lo), core: 2. Of those that a mesh axis runs over, the one named last changes fastest.
Arguments:
- inputs: bfloat16 [3, 512, 2304], P(None, 'rows', 'mp'), may hold values from -6 to 6
- gate_up: bfloat16 [3, 2304, 2, 9216], P(None, None, None, 'mp'), may hold values from -0.125 to 0.125
- down_weight: bfloat16 [3, 9216, 2304], P(None, 'mp'), may hold values from -0.1875 to 0.1875
- enc_weight: bfloat16 [3, 2304, 16384], P(None, None, 'mp'), may hold values from -0.125 to 0.125
- enc_bias: float32 [3, 16384], P(None, 'mp'), may hold values from -3 to 3
- dec_weight: bfloat16 [6, 16384, 2304], P(None, 'mp', 'rows'), may hold values from -0.1875 to 0.1875
Outputs:
- recon: float32 [3, 512, 2304], P(None, 'rows', 'mp')
- residual: float32 [3, 512, 2304], P(None, 'rows', 'mp')
All inputs are finite; a program needn't handle non-finite values.
Results may differ from a plain program's by a relative error of at most 0.0029.
Values may be sent and summed in bfloat16 or wider, within the bound.
No kernel may reach another device: no remote copies, remote signals or barrier semaphores. Data moves between devices by JAX's collectives and lax.ppermute only.
A program may use at most 128 MiB of HBM per device.

v0:
```python
import jax
import jax.numpy as jnp
from jax import lax
from jax.sharding import PartitionSpec as P


def joined_along(pieces, dim):
    pieces = jnp.moveaxis(pieces, 0, dim)
    lengths = pieces.shape
    return pieces.reshape(*lengths[:dim], lengths[dim] * lengths[dim + 1], *lengths[dim + 2 :])


def from_everyone(shard, axis):
    copies = jnp.broadcast_to(shard, (lax.axis_size(axis), *shard.shape))
    return lax.all_to_all(copies, axis, split_axis=0, concat_axis=0, tiled=True)


def gather_directly(shard, axis, dim):
    return joined_along(from_everyone(shard, axis), dim)


def cut_along(shard, dim, peers):
    lengths = shard.shape
    pieces = shard.reshape(*lengths[:dim], peers, lengths[dim] // peers, *lengths[dim + 1 :])
    return jnp.moveaxis(pieces, dim, 0)


def sum_at_owner(shard, axis, dim):
    pieces = cut_along(shard, dim, lax.axis_size(axis))
    arrived = lax.all_to_all(pieces, axis, split_axis=0, concat_axis=0, tiled=True)
    return arrived.sum(axis=0)


def encode(rows_in, joined, encoder):
    piece = gather_directly(rows_in, "mp", 1)
    return (
        jnp.dot(piece, joined, preferred_element_type=jnp.float32),
        jnp.dot(piece, encoder, preferred_element_type=jnp.float32),
    )


def body(inputs, gate_up, down_weight, enc_weight, enc_bias, dec_weight):
    layers = inputs.shape[0]
    model_width = gate_up.shape[1]
    hidden_local = gate_up.shape[3]
    targets = []
    latents = []
    for layer in range(layers):
        joined = gate_up[layer].reshape(model_width, 2 * hidden_local)
        mlp_pre, lat_pre = encode(inputs[layer], joined, enc_weight[layer])
        gate = mlp_pre[:, :hidden_local]
        upper = mlp_pre[:, hidden_local:]
        hidden = (jax.nn.gelu(gate, approximate=True) * upper).astype(jnp.bfloat16)
        partial_out = jnp.dot(hidden, down_weight[layer], preferred_element_type=jnp.float32)
        targets.append(sum_at_owner(partial_out, "mp", 1))
        latents.append(jax.nn.relu(lat_pre + enc_bias[layer][None, :]).astype(jnp.bfloat16))
    recons = []
    gathered = [gather_directly(latents[source], "rows", 0) for source in range(layers)]
    for target_layer in range(layers):
        summed = None
        for source in range(target_layer + 1):
            pair = target_layer * (target_layer + 1) // 2 + source
            term = jnp.dot(gathered[source], dec_weight[pair], preferred_element_type=jnp.float32)
            summed = term if summed is None else summed + term
        owned = lax.all_to_all(summed, "rows", split_axis=0, concat_axis=1, tiled=True)
        recons.append(sum_at_owner(owned, "mp", 1))
    recon = jnp.stack(recons)
    residual = jnp.stack(targets) - recon
    return (recon, residual)


def solution(mesh):
    in_specs = (
        P(None, "rows", "mp"),
        P(None, None, None, "mp"),
        P(None, "mp", None),
        P(None, None, "mp"),
        P(None, "mp"),
        P(None, "mp", "rows"),
    )
    out_specs = (P(None, "rows", "mp"), P(None, "rows", "mp"))
    return jax.shard_map(body, mesh=mesh, in_specs=in_specs, out_specs=out_specs, check_vma=False)
```

profile of v0, /device:TPU:4, one launch (start us, length us, event | category | flops | bytes accessed | tf_op | source)
XLA Modules:
  0.0 468.3 jit_solution(9627886158990245471)
XLA Ops:
  1.5 30.6 %all_to_all.105 = bf16[64,128,36]{1,2,0:T(8,128)(2,1)S(1)} all-to-all(bf16[64,128,36]{1,2,0:T(8,128)(2,1)S(1)} %broadcast_in_dim.22), channel_id=1, replica_groups=mesh['rows'=4,'mp'=64] {'mp'}, dimensions={0} | all-to-all | bytes 1179648 | tf_op jit(solution)/shard_map/all_to_all | solution.py:15
  32.1 24.9 %all_to_all.106 = bf16[64,128,36]{1,2,0:T(8,128)(2,1)S(1)} all-to-all(bf16[64,128,36]{1,2,0:T(8,128)(2,1)S(1)} %broadcast_in_dim.18), channel_id=1, replica_groups=mesh['rows'=4,'mp'=64] {'mp'}, dimensions={0} | all-to-all | bytes 1179648 | tf_op jit(solution)/shard_map/all_to_all | solution.py:15
  58.0 7.3 %all-to-all-start.4 = ((bf16[64,128,36]{1,2,0:T(8,128)(2,1)}), bf16[64,128,36]{1,2,0:T(8,128)(2,1)S(1)}, u32[]{:S(2)}, u32[]{:S(2)}) async-start(bf16[64,128,36]{1,2,0:T(8,128)(2,1)} %broadcast_in_dim.20), calls=%async_computation.4 | async-start | bytes 1310720 | tf_op jit(solution)/shard_map/all_to_all | solution.py:15
  67.3 15.7 %all-to-all-done.4 = bf16[64,128,36]{1,2,0:T(8,128)(2,1)S(1)} async-done(((bf16[64,128,36]{1,2,0:T(8,128)(2,1)}), bf16[64,128,36]{1,2,0:T(8,128)(2,1)S(1)}, u32[]{:S(2)}, u32[]{:S(2)}) %all-to-all-start.4) | async-done | bytes 589856 | tf_op jit(solution)/shard_map/all_to_all | solution.py:15
  91.5 8.0 %all-to-all-done.1 = bf16[4,128,256]{2,1,0:T(8,128)(2,1)S(1)} async-done(((bf16[4,128,256]{2,1,0:T(8,128)(2,1)}), bf16[4,128,256]{2,1,0:T(8,128)(2,1)S(1)}, u32[]{:S(2)}, u32[]{:S(2)}) %all-to-all-start.1) | async-done | bytes 262176 | tf_op jit(solution)/shard_map/all_to_all | solution.py:15
  105.6 10.7 %all-to-all-done.5 = bf16[4,128,256]{2,1,0:T(8,128)(2,1)S(1)} async-done(((bf16[4,128,256]{2,1,0:T(8,128)(2,1)}), bf16[4,128,256]{2,1,0:T(8,128)(2,1)S(1)}, u32[]{:S(2)}, u32[]{:S(2)}) %all-to-all-start.5) | async-done | bytes 262176 | tf_op jit(solution)/shard_map/all_to_all | solution.py:15
  123.1 7.4 %all-to-all-done.9 = bf16[4,128,256]{2,1,0:T(8,128)(2,1)S(1)} async-done(((bf16[4,128,256]{2,1,0:T(8,128)(2,1)}), bf16[4,128,256]{2,1,0:T(8,128)(2,1)S(1)}, u32[]{:S(2)}, u32[]{:S(2)}) %all-to-all-start.9) | async-done | bytes 262176 | tf_op jit(solution)/shard_map/all_to_all | solution.py:15
  140.1 28.6 %all-to-all-done.10 = f32[4,128,576]{1,2,0:T(8,128)S(1)} async-done(((f32[4,128,576]{1,2,0:T(8,128)}), f32[4,128,576]{1,2,0:T(8,128)S(1)}, u32[]{:S(2)}, u32[]{:S(2)}) %all-to-all-start.10) | async-done | bytes 1179680 | tf_op jit(solution)/shard_map/all_to_all | solution.py:65
  174.6 17.6 %all-to-all-done.6 = f32[4,128,576]{1,2,0:T(8,128)S(1)} async-done(((f32[4,128,576]{1,2,0:T(8,128)}), f32[4,128,576]{1,2,0:T(8,128)S(1)}, u32[]{:S(2)}, u32[]{:S(2)}) %all-to-all-start.6) | async-done | bytes 1179680 | tf_op jit(solution)/shard_map/all_to_all | solution.py:65
  199.3 6.4 %reshape.66 = bf16[64,36,144]{1,0,2:T(8,128)(2,1)S(1)} reshape(bf16[2304,144]{0,1:T(8,128)(2,1)S(1)} %get-tuple-element.8) | data formatting | bytes 1327104 | tf_op jit(solution)/shard_map/dot_general | solution.py:54
  217.4 20.8 %all-to-all-start.14 = ((f32[64,128,36]{1,2,0:T(8,128)}), f32[64,128,36]{1,2,0:T(8,128)}, u32[]{:S(2)}, u32[]{:S(2)}) async-start(f32[64,128,36]{1,2,0:T(8,128)} %copy.29), calls=%async_computation.14 | async-start | bytes 2621440 | tf_op jit(solution)/shard_map/all_to_all | solution.py:30
  238.3 6.4 %reshape.65 = bf16[64,36,144]{1,0,2:T(8,128)(2,1)S(1)} reshape(bf16[2304,144]{0,1:T(8,128)(2,1)S(1)} %copy-done.4) | data formatting | bytes 1327104 | tf_op jit(solution)/shard_map/dot_general | solution.py:54
  251.9 19.0 %all-to-all-done.14 = f32[64,128,36]{1,2,0:T(8,128)} async-done(((f32[64,128,36]{1,2,0:T(8,128)}), f32[64,128,36]{1,2,0:T(8,128)}, u32[]{:S(2)}, u32[]{:S(2)}) %all-to-all-start.14) | async-done | bytes 1179680 | tf_op jit(solution)/shard_map/all_to_all | solution.py:30
  270.9 8.0 %all-to-all-start.13 = ((f32[64,128,36]{1,2,0:T(8,128)}), f32[64,128,36]{1,2,0:T(8,128)}, u32[]{:S(2)}, u32[]{:S(2)}) async-start(f32[64,128,36]{1,2,0:T(8,128)} %copy.26), calls=%async_computation.13 | async-start | bytes 2621440 | tf_op jit(solution)/shard_map/all_to_all | solution.py:30
  278.9 6.4 %reshape.64 = bf16[64,36,144]{1,0,2:T(8,128)(2,1)S(1)} reshape(bf16[2304,144]{0,1:T(8,128)(2,1)S(1)} %copy-done.3) | data formatting | bytes 1327104 | tf_op jit(solution)/shard_map/dot_general | solution.py:54
  292.6 17.7 %all-to-all-done.13 = f32[64,128,36]{1,2,0:T(8,128)} async-done(((f32[64,128,36]{1,2,0:T(8,128)}), f32[64,128,36]{1,2,0:T(8,128)}, u32[]{:S(2)}, u32[]{:S(2)}) %all-to-all-start.13) | async-done | bytes 1179680 | tf_op jit(solution)/shard_map/all_to_all | solution.py:30
  310.3 7.2 %all-to-all-start.12 = ((f32[64,128,36]{1,2,0:T(8,128)}), f32[64,128,36]{1,2,0:T(8,128)S(1)}, u32[]{:S(2)}, u32[]{:S(2)}) async-start(f32[64,128,36]{1,2,0:T(8,128)} %copy.23), calls=%async_computation.12 | async-start | bytes 2621440 | tf_op jit(solution)/shard_map/all_to_all | solution.py:30
  318.6 30.4 %all-to-all-done.12 = f32[64,128,36]{1,2,0:T(8,128)S(1)} async-done(((f32[64,128,36]{1,2,0:T(8,128)}), f32[64,128,36]{1,2,0:T(8,128)S(1)}, u32[]{:S(2)}, u32[]{:S(2)}) %all-to-all-start.12) | async-done | bytes 1179680 | tf_op jit(solution)/shard_map/all_to_all | solution.py:30
  349.0 7.2 %all-to-all-start.11 = ((f32[64,128,36]{1,2,0:T(8,128)}), f32[64,128,36]{1,2,0:T(8,128)S(1)}, u32[]{:S(2)}, u32[]{:S(2)}) async-start(f32[64,128,36]{1,2,0:T(8,128)} %bitcast.153), calls=%async_computation.11 | async-start | bytes 2621440 | tf_op jit(solution)/shard_map/all_to_all | solution.py:30
  358.6 29.2 %all-to-all-done.11 = f32[64,128,36]{1,2,0:T(8,128)S(1)} async-done(((f32[64,128,36]{1,2,0:T(8,128)}), f32[64,128,36]{1,2,0:T(8,128)S(1)}, u32[]{:S(2)}, u32[]{:S(2)}) %all-to-all-start.11) | async-done | bytes 1179680 | tf_op jit(solution)/shard_map/all_to_all | solution.py:30
  387.7 8.2 %all-to-all-start.7 = ((f32[64,128,36]{1,2,0:T(8,128)}), f32[64,128,36]{1,2,0:T(8,128)}, u32[]{:S(2)}, u32[]{:S(2)}) async-start(f32[64,128,36]{1,2,0:T(8,128)} %bitcast.154), calls=%async_computation.7 | async-start | bytes 2621440 | tf_op jit(solution)/shard_map/all_to_all | solution.py:30
  398.3 28.8 %all-to-all-done.7 = f32[64,128,36]{1,2,0:T(8,128)} async-done(((f32[64,128,36]{1,2,0:T(8,128)}), f32[64,128,36]{1,2,0:T(8,128)}, u32[]{:S(2)}, u32[]{:S(2)}) %all-to-all-start.7) | async-done | bytes 1179680 | tf_op jit(solution)/shard_map/all_to_all | solution.py:30
  427.1 8.0 %all-to-all-start.3 = ((f32[64,128,36]{1,2,0:T(8,128)}), f32[64,128,36]{1,2,0:T(8,128)}, u32[]{:S(2)}, u32[]{:S(2)}) async-start(f32[64,128,36]{1,2,0:T(8,128)} %bitcast.152), calls=%async_computation.3 | async-start | bytes 2621440 | tf_op jit(solution)/shard_map/all_to_all | solution.py:30
  439.6 26.6 %all-to-all-done.3 = f32[64,128,36]{1,2,0:T(8,128)} async-done(((f32[64,128,36]{1,2,0:T(8,128)}), f32[64,128,36]{1,2,0:T(8,128)}, u32[]{:S(2)}, u32[]{:S(2)}) %all-to-all-start.3) | async-done | bytes 1179680 | tf_op jit(solution)/shard_map/all_to_all | solution.py:30
  (73 shorter events, 86.4 us)
Async XLA Ops:
  57.1 8.2 %copy-start.9 = (f32[3,256]{1,0:T(4,128)S(1)}, f32[3,256]{1,0:T(4,128)}, u32[]{:S(2)}) copy-start(f32[3,256]{1,0:T(4,128)} %param.10) | copy-start | bytes 9220
  58.0 25.0 %all-to-all-start.4 = ((bf16[64,128,36]{1,2,0:T(8,128)(2,1)}), bf16[64,128,36]{1,2,0:T(8,128)(2,1)S(1)}, u32[]{:S(2)}, u32[]{:S(2)}) async-start(bf16[64,128,36]{1,2,0:T(8,128)(2,1)} %broadcast_in_dim.20), calls=%async_computation.4 | async-start | bytes 1310720 | tf_op jit(solution)/shard_map/all_to_all | solution.py:15
  65.4 18.3 %copy-start.5 = (bf16[128,2304]{0,1:T(8,128)(2,1)}, bf16[128,2304]{0,1:T(8,128)(2,1)S(1)}, u32[]{:S(2)}) copy-start(bf16[128,2304]{0,1:T(8,128)(2,1)S(1)} %reshape.51) | copy-start | bytes 1769476
  83.7 15.8 %all-to-all-start.1 = ((bf16[4,128,256]{2,1,0:T(8,128)(2,1)}), bf16[4,128,256]{2,1,0:T(8,128)(2,1)S(1)}, u32[]{:S(2)}, u32[]{:S(2)}) async-start(bf16[4,128,256]{2,1,0:T(8,128)(2,1)} %broadcast_in_dim.19), calls=%async_computation.1 | async-start | bytes 524288 | tf_op jit(solution)/shard_map/all_to_all | solution.py:15
  89.6 10.6 %copy-start.6 = (bf16[128,2304]{0,1:T(8,128)(2,1)}, bf16[128,2304]{0,1:T(8,128)(2,1)S(1)}, u32[]{:S(2)}) copy-start(bf16[128,2304]{0,1:T(8,128)(2,1)S(1)} %reshape.54) | copy-start | bytes 1769476
  100.2 16.1 %all-to-all-start.5 = ((bf16[4,128,256]{2,1,0:T(8,128)(2,1)}), bf16[4,128,256]{2,1,0:T(8,128)(2,1)S(1)}, u32[]{:S(2)}, u32[]{:S(2)}) async-start(bf16[4,128,256]{2,1,0:T(8,128)(2,1)} %broadcast_in_dim.21), calls=%async_computation.5 | async-start | bytes 524288 | tf_op jit(solution)/shard_map/all_to_all | solution.py:15
  103.7 13.3 %copy-start.7 = (bf16[128,2304]{0,1:T(8,128)(2,1)}, bf16[128,2304]{0,1:T(8,128)(2,1)S(1)}, u32[]{:S(2)}) copy-start(bf16[128,2304]{0,1:T(8,128)(2,1)S(1)} %reshape.57) | copy-start | bytes 1769476
  117.1 13.4 %all-to-all-start.9 = ((bf16[4,128,256]{2,1,0:T(8,128)(2,1)}), bf16[4,128,256]{2,1,0:T(8,128)(2,1)S(1)}, u32[]{:S(2)}, u32[]{:S(2)}) async-start(bf16[4,128,256]{2,1,0:T(8,128)(2,1)} %broadcast_in_dim.23), calls=%async_computation.9 | async-start | bytes 524288 | tf_op jit(solution)/shard_map/all_to_all | solution.py:15
  132.9 35.9 %all-to-all-start.10 = ((f32[4,128,576]{1,2,0:T(8,128)}), f32[4,128,576]{1,2,0:T(8,128)S(1)}, u32[]{:S(2)}, u32[]{:S(2)}) async-start(f32[4,128,576]{1,2,0:T(8,128)} %bitcast.147), calls=%async_computation.10 | async-start | bytes 2359296 | tf_op jit(solution)/shard_map/all_to_all | solution.py:65
  168.8 5.9 %copy-start = (f32[4,128,576]{1,2,0:T(8,128)}, f32[4,128,576]{1,2,0:T(8,128)S(1)}, u32[]{:S(2)}) copy-start(f32[4,128,576]{1,2,0:T(8,128)S(1)} %all-to-all-done.10) | copy-start | bytes 3538948
  168.8 23.5 %all-to-all-start.6 = ((f32[4,128,576]{1,2,0:T(8,128)}), f32[4,128,576]{1,2,0:T(8,128)S(1)}, u32[]{:S(2)}, u32[]{:S(2)}) async-start(f32[4,128,576]{1,2,0:T(8,128)} %bitcast.148), calls=%async_computation.6 | async-start | bytes 2359296 | tf_op jit(solution)/shard_map/all_to_all | solution.py:65
  192.3 7.0 %copy-start.2 = (f32[4,128,576]{1,2,0:T(8,128)}, f32[4,128,576]{1,2,0:T(8,128)S(1)}, u32[]{:S(2)}) copy-start(f32[4,128,576]{1,2,0:T(8,128)S(1)} %all-to-all-done.6) | copy-start | bytes 3538948
  192.3 25.1 %all-to-all-start.2 = ((f32[4,128,576]{1,2,0:T(8,128)}), f32[4,128,576]{1,2,0:T(8,128)}, u32[]{:S(2)}, u32[]{:S(2)}) async-start(f32[4,128,576]{1,2,0:T(8,128)} %fusion.45), calls=%async_computation.2 | async-start | bytes 2359296 | tf_op jit(solution)/shard_map/all_to_all | solution.py:65
  208.7 4.0 copy-start.8
  215.4 22.8 %copy-start.4 = (bf16[2304,144]{0,1:T(8,128)(2,1)S(1)}, bf16[2304,144]{0,1:T(8,128)(2,1)}, u32[]{:S(2)}) copy-start(bf16[2304,144]{0,1:T(8,128)(2,1)} %get-tuple-element.9) | copy-start | bytes 1990660
  217.4 53.5 %all-to-all-start.14 = ((f32[64,128,36]{1,2,0:T(8,128)}), f32[64,128,36]{1,2,0:T(8,128)}, u32[]{:S(2)}, u32[]{:S(2)}) async-start(f32[64,128,36]{1,2,0:T(8,128)} %copy.29), calls=%async_computation.14 | async-start | bytes 2621440 | tf_op jit(solution)/shard_map/all_to_all | solution.py:30
  251.9 27.0 %copy-start.3 = (bf16[2304,144]{0,1:T(8,128)(2,1)S(1)}, bf16[2304,144]{0,1:T(8,128)(2,1)}, u32[]{:S(2)}) copy-start(bf16[2304,144]{0,1:T(8,128)(2,1)} %get-tuple-element.7) | copy-start | bytes 1990660
  270.9 39.3 %all-to-all-start.13 = ((f32[64,128,36]{1,2,0:T(8,128)}), f32[64,128,36]{1,2,0:T(8,128)}, u32[]{:S(2)}, u32[]{:S(2)}) async-start(f32[64,128,36]{1,2,0:T(8,128)} %copy.26), calls=%async_computation.13 | async-start | bytes 2621440 | tf_op jit(solution)/shard_map/all_to_all | solution.py:30
  292.6 24.9 %copy-start.1 = (f32[4,128,576]{1,2,0:T(8,128)S(1)}, f32[4,128,576]{1,2,0:T(8,128)}, u32[]{:S(2)}) copy-start(f32[4,128,576]{1,2,0:T(8,128)} %copy-done) | copy-start | bytes 3538948
  310.3 38.7 %all-to-all-start.12 = ((f32[64,128,36]{1,2,0:T(8,128)}), f32[64,128,36]{1,2,0:T(8,128)S(1)}, u32[]{:S(2)}, u32[]{:S(2)}) async-start(f32[64,128,36]{1,2,0:T(8,128)} %copy.23), calls=%async_computation.12 | async-start | bytes 2621440 | tf_op jit(solution)/shard_map/all_to_all | solution.py:30
  349.0 38.7 %all-to-all-start.11 = ((f32[64,128,36]{1,2,0:T(8,128)}), f32[64,128,36]{1,2,0:T(8,128)S(1)}, u32[]{:S(2)}, u32[]{:S(2)}) async-start(f32[64,128,36]{1,2,0:T(8,128)} %bitcast.153), calls=%async_computation.11 | async-start | bytes 2621440 | tf_op jit(solution)/shard_map/all_to_all | solution.py:30
  387.7 39.4 %all-to-all-start.7 = ((f32[64,128,36]{1,2,0:T(8,128)}), f32[64,128,36]{1,2,0:T(8,128)}, u32[]{:S(2)}, u32[]{:S(2)}) async-start(f32[64,128,36]{1,2,0:T(8,128)} %bitcast.154), calls=%async_computation.7 | async-start | bytes 2621440 | tf_op jit(solution)/shard_map/all_to_all | solution.py:30
  427.1 39.1 %all-to-all-start.3 = ((f32[64,128,36]{1,2,0:T(8,128)}), f32[64,128,36]{1,2,0:T(8,128)}, u32[]{:S(2)}, u32[]{:S(2)}) async-start(f32[64,128,36]{1,2,0:T(8,128)} %bitcast.152), calls=%async_computation.3 | async-start | bytes 2621440 | tf_op jit(solution)/shard_map/all_to_all | solution.py:30
where the time goes:
time: 472 us; the launch traced here: 468 us
  waiting for transfers between devices  242 us (51%)
  starting transfers between devices  90.5 us (19%)
  blocking collectives  55.5 us (12%)
  local copies, waits for them, and re-layouts  52.7 us (11%)
  matrix products  20.4 us (4%)
  other arithmetic  6.6 us (1%)
    all_to_all x6, waiting for transfers between devices, sum_at_owner(): lax.all_to_all(pieces, axis, split_axis=0, concat_axis=0, tiled=True)  152 us
    all_to_all x6, starting transfers between devices, sum_at_owner(): lax.all_to_all(pieces, axis, split_axis=0, concat_axis=0, tiled=True)  59.4 us
    all_to_all x2, blocking collectives, from_everyone(): return lax.all_to_all(copies, axis, split_axis=0, concat_axis=0, tiled=True)  55.5 us
    all_to_all x3, waiting for transfers between devices, body(): lax.all_to_all(summed, 'rows', split_axis=0, concat_axis=1, tiled=True)  48.3 us
    all_to_all x4, waiting for transfers between devices, from_everyone(): return lax.all_to_all(copies, axis, split_axis=0, concat_axis=0, tiled=True)  41.7 us
    dot_general x7, local copies, waits for them, and re-layouts, body(): jnp.dot(hidden, down_weight[layer], preferred_element_type=jnp.float32)  30.9 us
    all_to_all x4, starting transfers between devices, from_everyone(): return lax.all_to_all(copies, axis, split_axis=0, concat_axis=0, tiled=True)  19.8 us
    all_to_all x3, starting transfers between devices, body(): lax.all_to_all(summed, 'rows', split_axis=0, concat_axis=1, tiled=True)  11.3 us
  transfers between devices with their start and end apart: 13, of which 13 were waited for; matrix products, arithmetic and copies ran while one was open for 15% of the time, Pallas kernels for 0%

commit v1 on v0

v1 whole, which is shorter than its diff:
```python
import jax
import jax.numpy as jnp
from jax import lax
from jax.sharding import Mesh, PartitionSpec as P

BF16 = jnp.bfloat16
F32 = jnp.float32
ROWS = ("zh", "core")
PLANE = ("x", "y")
LAYERS = 3


def exchange(pieces, axis):
    return lax.all_to_all(pieces, axis, split_axis=0, concat_axis=0, tiled=True)


def from_everyone(shard, axis):
    count = lax.axis_size(axis)
    return exchange(jnp.broadcast_to(shard, (count, *shard.shape)), axis)


def body(inputs, gate_up, down_weight, enc_weight, enc_bias, dec_weight):
    layers, rows, width = inputs.shape
    hidden = gate_up.shape[3]
    model = gate_up.shape[1]
    mine = jnp.swapaxes(inputs, 1, 2)
    run = from_everyone(mine, "zl")
    run = jnp.moveaxis(run, 0, 1).reshape(layers, 4 * width, rows)
    everything = from_everyone(run, PLANE)
    features = jnp.moveaxis(everything, 0, 1).reshape(layers, model, rows)

    latents = []
    for layer in range(layers):
        pre = jnp.einsum("dk,dn->kn", enc_weight[layer], features[layer], preferred_element_type=F32)
        latents.append(jax.nn.relu(pre + enc_bias[layer][:, None]).astype(BF16))
    gathered = lax.all_gather(jnp.stack(latents), ROWS, axis=0)

    joined = jnp.transpose(gate_up, (0, 2, 3, 1)).reshape(layers, 2 * hidden, model)
    sums = []
    for layer in range(layers):
        pre = jnp.einsum("jd,dn->jn", joined[layer], features[layer], preferred_element_type=F32)
        act = (jax.nn.gelu(pre[:hidden], approximate=True) * pre[hidden:]).astype(BF16)
        out = jnp.einsum("kf,kn->fn", down_weight[layer], act, preferred_element_type=F32)
        sums.append(out.astype(BF16))
    decoder = jnp.swapaxes(dec_weight, 1, 2)
    for target in range(layers):
        total = None
        for source in range(target + 1):
            pair = target * (target + 1) // 2 + source
            term = jnp.einsum("fk,rkn->rfn", decoder[pair], gathered[:, source], preferred_element_type=F32)
            total = term if total is None else total + term
        sums.append(total.reshape(model, rows).astype(BF16))
    pieces = jnp.stack(sums).reshape(2 * layers, 16, 4 * width, rows)
    arrived = exchange(jnp.moveaxis(pieces, 1, 0), PLANE)
    partial = arrived.astype(F32).sum(axis=0)
    partial = jnp.moveaxis(partial.reshape(2 * layers, 4, width, rows), 1, 0)
    owned = exchange(partial, "zl").sum(axis=0)
    swap = []
    for row in range(4):
        for place in range(4):
            swap.append((row * 4 + place, place * 4 + row))
    recon = lax.ppermute(owned[layers:], ("zh", "core", "x"), swap)
    residual = owned[:layers] - recon
    return jnp.swapaxes(recon, 1, 2), jnp.swapaxes(residual, 1, 2)


def solution(mesh):
    fine = Mesh(mesh.devices.reshape(2, 2, 4, 4, 4), ("zh", "core", "x", "y", "zl"))
    mp = ("x", "y", "zl")
    in_specs = (
        P(None, ROWS, mp),
        P(None, None, None, mp),
        P(None, mp, None),
        P(None, None, mp),
        P(None, mp),
        P(None, mp, ROWS),
    )
    out_specs = (P(None, ROWS, mp), P(None, ROWS, mp))
    return jax.shard_map(body, mesh=fine, in_specs=in_specs, out_specs=out_specs, check_vma=False)
```

time: 472 us -> 156 us (0.33)
  waiting for transfers between devices: 242 us -> 23.9 us
  starting transfers between devices: 90.5 us -> 13.6 us
  local copies, waits for them, and re-layouts: 52.7 us -> 12.2 us
  blocking collectives: 55.5 us -> 92.3 us
  matrix products: 20.4 us -> 11.7 us
  other arithmetic: 6.6 us -> 1.22 us
    all_to_all x13 -> x1, waiting for transfers between devices: 242 us -> 17.4 us  [exchange(): return lax.all_to_all(pieces, axis, split_axis=0, concat_axis=0, tiled=True)]
    all_to_all x13 -> x1, starting transfers between devices: 90.5 us -> 7.58 us  [exchange(): return lax.all_to_all(pieces, axis, split_axis=0, concat_axis=0, tiled=True)]
    dot_general x7 -> x0, local copies, waits for them, and re-layouts: 30.9 us -> none  [body(): jnp.dot(hidden, down_weight[layer], preferred_element_type=jnp.float32)]
    all_to_all x2 -> x3, blocking collectives: 55.5 us -> 77.3 us  [exchange(): return lax.all_to_all(pieces, axis, split_axis=0, concat_axis=0, tiled=True)]
    all_gather x0 -> x1, blocking collectives: none -> 15.1 us  [body(): gathered = lax.all_gather(jnp.stack(latents), ROWS, axis=0)]
    dot_general x15, matrix products: 20.4 us -> 11.7 us  [the longest x3 5.37 us: body(): jnp.einsum('kf,kn->fn', down_weight[layer], act, preferred_element_type=F32)]
    ppermute x0 -> x1, waiting for transfers between devices: none -> 6.51 us  [body(): recon = lax.ppermute(owned[layers:], ('zh', 'core', 'x'), swap)]
    reshape x6 -> x2, local copies, waits for them, and re-layouts: 6.26 us -> 0.06 us  [the longest x1 0.03 us: body(): partial = jnp.moveaxis(partial.reshape(2 * layers, 4, width, rows), 1, 0)]
  transfers between devices with their start and end apart: 13 -> 2, of which waited for: 13 -> 2; matrix products, arithmetic and copies ran while one was open for 15% -> 2% of each run, Pallas kernels for 0% -> 0%
where the time goes in v1:
time: 156 us
  blocking collectives  92.3 us (59%)
  waiting for transfers between devices  23.9 us (15%)
  starting transfers between devices  13.6 us (9%)
  local copies, waits for them, and re-layouts  12.2 us (8%)
  matrix products  11.7 us (8%)
    all_to_all x3, blocking collectives, exchange(): return lax.all_to_all(pieces, axis, split_axis=0, concat_axis=0, tiled=True)  77.3 us
    all_to_all x1, waiting for transfers between devices, exchange(): return lax.all_to_all(pieces, axis, split_axis=0, concat_axis=0, tiled=True)  17.4 us
    all_gather x1, blocking collectives, body(): gathered = lax.all_gather(jnp.stack(latents), ROWS, axis=0)  15.1 us
    all_to_all x1, starting transfers between devices, exchange(): return lax.all_to_all(pieces, axis, split_axis=0, concat_axis=0, tiled=True)  7.58 us
    ppermute x1, waiting for transfers between devices, body(): recon = lax.ppermute(owned[layers:], ('zh', 'core', 'x'), swap)  6.51 us
    ppermute x1, starting transfers between devices, body(): recon = lax.ppermute(owned[layers:], ('zh', 'core', 'x'), swap)  6.04 us
    dot_general x3, matrix products, body(): jnp.einsum('kf,kn->fn', down_weight[layer], act, preferred_element_type=F32)  5.37 us
    slice x1, local copies, waits for them, and re-layouts, body(): joined[layer]  3.87 us
  transfers between devices with their start and end apart: 2, of which 2 were waited for; matrix products, arithmetic and copies ran while one was open for 2% of the time, Pallas kernels for 0%

profile of v1, /device:TPU:4, one launch (start us, length us, event | category | flops | bytes accessed | tf_op | source)
XLA Modules:
  0.0 155.7 jit_solution(12864669411370911069)
XLA Ops:
  0.6 0.8 broadcast_in_dim.6
  1.4 11.7 %all_to_all.20 = bf16[4,3,36,128]{3,2,1,0:T(8,128)(2,1)S(1)} all-to-all(bf16[4,3,36,128]{3,2,1,0:T(8,128)(2,1)S(1)} %broadcast_in_dim.6), channel_id=1, replica_groups=mesh['zh'=2,'core'=2,'x'=4,'y'=4,'zl'=4] {'zl'}, dimensions={0} | all-to-all | bytes 221184 | tf_op jit(solution)/shard_map/all_to_all | solution.py:14
  13.1 1.5 broadcast_in_dim.7
  14.6 7.6 %all-to-all-start.1 = ((bf16[16,3,144,128]{3,2,1,0:T(8,128)(2,1)}), bf16[16,3,144,128]{3,2,1,0:T(8,128)(2,1)S(1)}, u32[]{:S(2)}, u32[]{:S(2)}) async-start(bf16[16,3,144,128]{3,2,1,0:T(8,128)(2,1)} %broadcast_in_dim.7), calls=%async_computation.1 | async-start | bytes 3538944 | tf_op jit(solution)/shard_map/all_to_all | solution.py:14
  22.2 3.9 %fusion.113 = (bf16[1,2,144,2304]{3,2,1,0:T(8,128)(2,1)}, bf16[1,2,144,2304]{3,2,1,0:T(8,128)(2,1)S(1)}, bf16[1,2,144,2304]{3,2,1,0:T(8,128)(2,1)}) fusion(bf16[3,2,144,2304]{3,2,1,0:T(8,128)(2,1)} %bitcast.148), kind=kLoop, calls=%fused_computation.114 | loop fusion | bytes 7962624 | tf_op jit(solution)/shard_map/slice | solution.py:41
  26.1 17.4 %all-to-all-done.1 = bf16[16,3,144,128]{3,2,1,0:T(8,128)(2,1)S(1)} async-done(((bf16[16,3,144,128]{3,2,1,0:T(8,128)(2,1)}), bf16[16,3,144,128]{3,2,1,0:T(8,128)(2,1)S(1)}, u32[]{:S(2)}, u32[]{:S(2)}) %all-to-all-start.1) | async-done | bytes 1769504 | tf_op jit(solution)/shard_map/all_to_all | solution.py:14
  43.6 1.9 %copy-done.4 = bf16[3,2304,256]{2,1,0:T(8,128)(2,1)S(1)} copy-done((bf16[3,2304,256]{2,1,0:T(8,128)(2,1)S(1)}, bf16[3,2304,256]{2,1,0:T(8,128)(2,1)}, u32[]{:S(2)}) %copy-start.4) | copy-done | bytes 3538968
  46.0 0.5 fusion.47
  46.5 0.5 fusion.41
  47.0 15.1 %all-gather = bf16[12,256,128]{2,1,0:T(8,128)(2,1)S(1)} all-gather(bf16[3,256,128]{2,1,0:T(8,128)(2,1)S(1)} %pad_maximum_fusion), channel_id=2, replica_groups=mesh['zh'=2,'core'=2,'x'=4,'y'=4,'zl'=4] {'zh','core'}, dimensions={0}, use_global_device_ids=true | all-gather | bytes 983040 | tf_op jit(solution)/shard_map/all_gather | solution.py:36
  64.1 0.7 copy-done.1
  64.7 1.2 fusion.116
  65.9 1.2 fusion.118
  67.6 1.5 fusion.1
  69.3 1.5 fusion.2
  71.2 2.4 %fusion = bf16[2304,128]{0,1:T(8,128)(2,1)} fusion(bf16[3,144,2304]{2,1,0:T(8,128)(2,1)} %param.8, f32[288,128]{1,0:T(8,128)} %fusion.116), kind=kOutput, calls=%fused_computation.4 | convolution fusion | flops 85413888 | bytes 1400832 | tf_op jit(solution)/shard_map/kf,kn->fn/dot_general | solution.py:43
  73.6 1.4 copy.27
  75.7 49.0 %all_to_all.21 = bf16[16,6,144,128]{3,2,1,0:T(8,128)(2,1)S(1)} all-to-all(bf16[16,6,144,128]{3,2,1,0:T(8,128)(2,1)S(1)} %copy.33), channel_id=1, replica_groups=mesh['zh'=2,'core'=2,'x'=4,'y'=4,'zl'=4] {'x','y'}, dimensions={0} | all-to-all | bytes 7077888 | tf_op jit(solution)/shard_map/all_to_all | solution.py:14
  124.6 0.5 convert_reduce_fusion
  125.2 16.6 %all_to_all.22 = f32[4,6,36,128]{3,2,1,0:T(8,128)S(1)} all-to-all(f32[4,6,36,128]{3,2,1,0:T(8,128)S(1)} %copy.34), channel_id=1, replica_groups=mesh['zh'=2,'core'=2,'x'=4,'y'=4,'zl'=4] {'zl'}, dimensions={0} | all-to-all | bytes 884736 | tf_op jit(solution)/shard_map/all_to_all | solution.py:14
  141.9 6.0 %collective-permute-start = (f32[3,36,128]{2,1,0:T(8,128)S(1)}, f32[3,36,128]{2,1,0:T(8,128)S(1)}, u32[]{:S(2)}, u32[]{:S(2)}) collective-permute-start(f32[3,36,128]{2,1,0:T(8,128)S(1)} %slice.161), channel_id=1, source_target_pairs={{0,0},{16,64},{32,128},{48,192},{64,16},{80,80},{96,144},{112,208}... | collective-permute-start | bytes 165896 | tf_op jit(solution)/shard_map/ppermute | solution.py:62
  147.9 6.5 %collective-permute-done = f32[3,36,128]{2,1,0:T(8,128)S(1)} collective-permute-done((f32[3,36,128]{2,1,0:T(8,128)S(1)}, f32[3,36,128]{2,1,0:T(8,128)S(1)}, u32[]{:S(2)}, u32[]{:S(2)}) %collective-permute-start) | collective-permute-done | bytes 55328 | tf_op jit(solution)/shard_map/ppermute | solution.py:62
  154.5 0.6 fusion.85
  155.1 0.6 copy.44
  (34 shorter events, 4.5 us)
Async XLA Ops:
  14.6 7.6 %copy-start.3 = (f32[3,256]{1,0:T(4,128)S(1)}, f32[3,256]{1,0:T(4,128)}, u32[]{:S(2)}) copy-start(f32[3,256]{1,0:T(4,128)} %param.10) | copy-start | bytes 9220
  14.6 28.8 %all-to-all-start.1 = ((bf16[16,3,144,128]{3,2,1,0:T(8,128)(2,1)}), bf16[16,3,144,128]{3,2,1,0:T(8,128)(2,1)S(1)}, u32[]{:S(2)}, u32[]{:S(2)}) async-start(bf16[16,3,144,128]{3,2,1,0:T(8,128)(2,1)} %broadcast_in_dim.7), calls=%async_computation.1 | async-start | bytes 3538944 | tf_op jit(solution)/shard_map/all_to_all | solution.py:14
  43.4 2.0 %copy-start.4 = (bf16[3,2304,256]{2,1,0:T(8,128)(2,1)S(1)}, bf16[3,2304,256]{2,1,0:T(8,128)(2,1)}, u32[]{:S(2)}) copy-start(bf16[3,2304,256]{2,1,0:T(8,128)(2,1)} %param.9) | copy-start | bytes 10616836
  46.5 15.6 %copy-start.2 = (bf16[6,256,576]{1,2,0:T(8,128)(2,1)S(1)}, bf16[6,256,576]{1,2,0:T(8,128)(2,1)}, u32[]{:S(2)}) copy-start(bf16[6,256,576]{1,2,0:T(8,128)(2,1)} %param.11) | copy-start | bytes 5308420
  63.4 1.3 copy-start.1
  63.7 2.2 %copy-start = (bf16[1,2,144,2304]{3,2,1,0:T(8,128)(2,1)S(1)}, bf16[1,2,144,2304]{3,2,1,0:T(8,128)(2,1)}, u32[]{:S(2)}) copy-start(bf16[1,2,144,2304]{3,2,1,0:T(8,128)(2,1)} %get-tuple-element.2) | copy-start | bytes 3981316
  141.9 12.6 %collective-permute-start = (f32[3,36,128]{2,1,0:T(8,128)S(1)}, f32[3,36,128]{2,1,0:T(8,128)S(1)}, u32[]{:S(2)}, u32[]{:S(2)}) collective-permute-start(f32[3,36,128]{2,1,0:T(8,128)S(1)} %slice.161), channel_id=1, source_target_pairs={{0,0},{16,64},{32,128},{48,192},{64,16},{80,80},{96,144},{112,208}... | collective-permute-start | bytes 165896 | tf_op jit(solution)/shard_map/ppermute | solution.py:62

commit v2 on v1

--- a/solution.py
+++ b/solution.py
@@ -19,6 +19,28 @@
     return exchange(jnp.broadcast_to(shard, (count, *shard.shape)), axis)
 
 
+def plane_exchange(parts, width):
+    layers, model, rows = parts.shape
+    return exchange(jnp.moveaxis(parts.reshape(layers, 16, 4 * width, rows), 1, 0), PLANE)
+
+
+def plane_sum(arrived, width):
+    layers, rows = arrived.shape[1], arrived.shape[3]
+    partial = arrived.astype(F32).sum(axis=0)
+    return jnp.moveaxis(partial.reshape(layers, 4, width, rows), 1, 0)
+
+
+def permuted_sum(pieces, axis):
+    here = lax.axis_index(axis)
+    count = pieces.shape[0]
+    total = lax.dynamic_index_in_dim(pieces, here, 0, False)
+    for step in range(1, count):
+        ring = [(index, (index + step) % count) for index in range(count)]
+        piece = lax.dynamic_index_in_dim(pieces, (here + step) % count, 0, False)
+        total = total + lax.ppermute(piece, axis, ring)
+    return total
+
+
 def body(inputs, gate_up, down_weight, enc_weight, enc_bias, dec_weight):
     layers, rows, width = inputs.shape
     hidden = gate_up.shape[3]
@@ -36,12 +58,13 @@
     gathered = lax.all_gather(jnp.stack(latents), ROWS, axis=0)
 
     joined = jnp.transpose(gate_up, (0, 2, 3, 1)).reshape(layers, 2 * hidden, model)
-    sums = []
+    targets = []
     for layer in range(layers):
         pre = jnp.einsum("jd,dn->jn", joined[layer], features[layer], preferred_element_type=F32)
         act = (jax.nn.gelu(pre[:hidden], approximate=True) * pre[hidden:]).astype(BF16)
         out = jnp.einsum("kf,kn->fn", down_weight[layer], act, preferred_element_type=F32)
-        sums.append(out.astype(BF16))
+        targets.append(out.astype(BF16))
+    recons = []
     decoder = jnp.swapaxes(dec_weight, 1, 2)
     for target in range(layers):
         total = None
@@ -49,18 +72,19 @@
             pair = target * (target + 1) // 2 + source
             term = jnp.einsum("fk,rkn->rfn", decoder[pair], gathered[:, source], preferred_element_type=F32)
             total = term if total is None else total + term
-        sums.append(total.reshape(model, rows).astype(BF16))
-    pieces = jnp.stack(sums).reshape(2 * layers, 16, 4 * width, rows)
-    arrived = exchange(jnp.moveaxis(pieces, 1, 0), PLANE)
-    partial = arrived.astype(F32).sum(axis=0)
-    partial = jnp.moveaxis(partial.reshape(2 * layers, 4, width, rows), 1, 0)
-    owned = exchange(partial, "zl").sum(axis=0)
+        recons.append(total.reshape(model, rows).astype(BF16))
+    first = plane_exchange(jnp.stack(recons), width)
+    outs, first = lax.optimization_barrier((jnp.stack(targets), first))
+    second = plane_exchange(outs, width)
+    recon = permuted_sum(plane_sum(first, width), "zl")
     swap = []
     for row in range(4):
         for place in range(4):
             swap.append((row * 4 + place, place * 4 + row))
-    recon = lax.ppermute(owned[layers:], ("zh", "core", "x"), swap)
-    residual = owned[:layers] - recon
+    recon = lax.ppermute(recon, ("zh", "core", "x"), swap)
+    second, recon = lax.optimization_barrier((second, recon))
+    target = exchange(plane_sum(second, width), "zl").sum(axis=0)
+    residual = target - recon
     return jnp.swapaxes(recon, 1, 2), jnp.swapaxes(residual, 1, 2)
 
 

time: 156 us -> 146 us (0.936)
  blocking collectives: 92.3 us -> 26.7 us
  waiting for transfers between devices: 23.9 us -> 59.1 us
  starting transfers between devices: 13.6 us -> 33.1 us
  matrix products: 11.7 us -> 7.32 us
  other arithmetic: 1.22 us -> 4.28 us
    all_to_all x3 -> x1, blocking collectives: 77.3 us -> 11.7 us  [exchange(): return lax.all_to_all(pieces, axis, split_axis=0, concat_axis=0, tiled=True)]
    all_to_all x1 -> x4, waiting for transfers between devices: 17.4 us -> 45.8 us  [exchange(): return lax.all_to_all(pieces, axis, split_axis=0, concat_axis=0, tiled=True)]
    all_to_all x1 -> x4, starting transfers between devices: 7.58 us -> 25.5 us  [exchange(): return lax.all_to_all(pieces, axis, split_axis=0, concat_axis=0, tiled=True)]
    ppermute x1 -> x4, waiting for transfers between devices: 6.51 us -> 13.3 us  [the longest x1 7.95 us: body(): recon = lax.ppermute(recon, ('zh', 'core', 'x'), swap)]
    dot_general x3, matrix products: 5.37 us -> 2.35 us  [body(): jnp.einsum('kf,kn->fn', down_weight[layer], act, preferred_element_type=F32)]
    convert_element_type x3 -> x0, local copies, waits for them, and re-layouts: 1.97 us -> none  [body(): sums.append(out.astype(BF16))]
    transpose x2, local copies, waits for them, and re-layouts: 0.26 us -> 2.04 us  [the longest x1 1.34 us: plane_exchange(): jnp.moveaxis(parts.reshape(layers, 16, 4 * width, rows), 1, 0)]
    ppermute x1 -> x4, starting transfers between devices: 6.04 us -> 7.55 us  [the longest x1 4.47 us: body(): recon = lax.ppermute(recon, ('zh', 'core', 'x'), swap)]
  transfers between devices with their start and end apart: 2 -> 8, of which waited for: 2 -> 8; matrix products, arithmetic and copies ran while one was open for 2% -> 7% of each run, Pallas kernels for 0% -> 0%
where the time goes in v2:
time: 146 us; the launch traced here: 144 us
  waiting for transfers between devices  59.1 us (40%)
  starting transfers between devices  33.1 us (23%)
  blocking collectives  26.7 us (18%)
  local copies, waits for them, and re-layouts  12.8 us (9%)
  matrix products  7.32 us (5%)
  other arithmetic  4.28 us (3%)
    all_to_all x4, waiting for transfers between devices, exchange(): return lax.all_to_all(pieces, axis, split_axis=0, concat_axis=0, tiled=True)  45.8 us
    all_to_all x4, starting transfers between devices, exchange(): return lax.all_to_all(pieces, axis, split_axis=0, concat_axis=0, tiled=True)  25.5 us
    all_gather x1, blocking collectives, body(): gathered = lax.all_gather(jnp.stack(latents), ROWS, axis=0)  15.1 us
    all_to_all x1, blocking collectives, exchange(): return lax.all_to_all(pieces, axis, split_axis=0, concat_axis=0, tiled=True)  11.7 us
    ppermute x1, waiting for transfers between devices, body(): recon = lax.ppermute(recon, ('zh', 'core', 'x'), swap)  7.95 us
    ppermute x3, waiting for transfers between devices, permuted_sum(): total = total + lax.ppermute(piece, axis, ring)  5.36 us
    ppermute x1, starting transfers between devices, body(): recon = lax.ppermute(recon, ('zh', 'core', 'x'), swap)  4.47 us
    slice x1, local copies, waits for them, and re-layouts, body(): joined[layer]  3.87 us
  transfers between devices with their start and end apart: 8, of which 8 were waited for; matrix products, arithmetic and copies ran while one was open for 7% of the time, Pallas kernels for 0%

profile of v2, /device:TPU:4, one launch (start us, length us, event | category | flops | bytes accessed | tf_op | source)
XLA Modules:
  0.0 144.3 jit_solution(3911577029372056737)
XLA Ops:
  1.4 11.7 %all_to_all.25 = bf16[4,3,36,128]{3,2,1,0:T(8,128)(2,1)S(1)} all-to-all(bf16[4,3,36,128]{3,2,1,0:T(8,128)(2,1)S(1)} %broadcast_in_dim.6), channel_id=1, replica_groups=mesh['zh'=2,'core'=2,'x'=4,'y'=4,'zl'=4] {'zl'}, dimensions={0} | all-to-all | bytes 221184 | tf_op jit(solution)/shard_map/all_to_all | solution.py:14
  13.1 1.5 %broadcast_in_dim.7 = bf16[16,3,144,128]{3,2,1,0:T(8,128)(2,1)} broadcast(bf16[3,144,128]{2,1,0:T(8,128)(2,1)S(1)} %reshape.84), dimensions={1,2,3} | broadcast | bytes 1880064 | tf_op jit(solution)/shard_map/broadcast_in_dim | solution.py:19
  14.6 7.6 %all-to-all-start.1 = ((bf16[16,3,144,128]{3,2,1,0:T(8,128)(2,1)}), bf16[16,3,144,128]{3,2,1,0:T(8,128)(2,1)S(1)}, u32[]{:S(2)}, u32[]{:S(2)}) async-start(bf16[16,3,144,128]{3,2,1,0:T(8,128)(2,1)} %broadcast_in_dim.7), calls=%async_computation.1 | async-start | bytes 3538944 | tf_op jit(solution)/shard_map/all_to_all | solution.py:14
  22.2 3.9 %fusion.114 = (bf16[1,2,144,2304]{3,2,1,0:T(8,128)(2,1)S(1)}, bf16[1,2,144,2304]{3,2,1,0:T(8,128)(2,1)}, bf16[1,2,144,2304]{3,2,1,0:T(8,128)(2,1)}) fusion(bf16[3,2,144,2304]{3,2,1,0:T(8,128)(2,1)} %bitcast.173), kind=kLoop, calls=%fused_computation.116 | loop fusion | bytes 7962624 | tf_op jit(solution)/shard_map/slice | solution.py:63
  26.1 17.4 %all-to-all-done.1 = bf16[16,3,144,128]{3,2,1,0:T(8,128)(2,1)S(1)} async-done(((bf16[16,3,144,128]{3,2,1,0:T(8,128)(2,1)}), bf16[16,3,144,128]{3,2,1,0:T(8,128)(2,1)S(1)}, u32[]{:S(2)}, u32[]{:S(2)}) %all-to-all-start.1) | async-done | bytes 1769504 | tf_op jit(solution)/shard_map/all_to_all | solution.py:14
  43.6 2.5 %copy-done.11 = bf16[3,2304,256]{2,1,0:T(8,128)(2,1)S(1)} copy-done((bf16[3,2304,256]{2,1,0:T(8,128)(2,1)S(1)}, bf16[3,2304,256]{2,1,0:T(8,128)(2,1)}, u32[]{:S(2)}) %copy-start.11) | copy-done | bytes 3538968
  47.7 15.1 %all-gather = bf16[12,256,128]{2,1,0:T(8,128)(2,1)S(1)} all-gather(bf16[3,256,128]{2,1,0:T(8,128)(2,1)S(1)} %pad_maximum_fusion.1), channel_id=2, replica_groups=mesh['zh'=2,'core'=2,'x'=4,'y'=4,'zl'=4] {'zh','core'}, dimensions={0}, use_global_device_ids=true | all-gather | bytes 983040 | tf_op jit(solution)/shard_map/all_gather | solution.py:58
  64.7 1.4 maximum_bitcast_fusion
  66.1 7.6 %all-to-all-start.2 = ((bf16[16,3,144,128]{3,2,1,0:T(8,128)(2,1)}), bf16[16,3,144,128]{3,2,1,0:T(8,128)(2,1)}, u32[]{:S(2)}, u32[]{:S(2)}) async-start(bf16[16,3,144,128]{3,2,1,0:T(8,128)(2,1)} %maximum_bitcast_fusion), calls=%async_computation.2 | async-start | bytes 3538944 | tf_op jit(solution)/shard_map/all_to_all | solution.py:14
  74.3 1.6 %fusion.2 = bf16[1,2304,128]{1,2,0:T(8,128)(2,1)S(1)} fusion(bf16[3,144,2304]{2,1,0:T(8,128)(2,1)} %param.8, f32[288,128]{1,0:T(8,128)S(1)} %fusion.119), kind=kOutput, calls=%fused_computation.7 | convolution fusion | flops 85413888 | bytes 1400832 | tf_op jit(solution)/shard_map/kf,kn->fn/dot_general | solution.py:65
  78.1 20.8 %all-to-all-done.2 = bf16[16,3,144,128]{3,2,1,0:T(8,128)(2,1)} async-done(((bf16[16,3,144,128]{3,2,1,0:T(8,128)(2,1)}), bf16[16,3,144,128]{3,2,1,0:T(8,128)(2,1)}, u32[]{:S(2)}, u32[]{:S(2)}) %all-to-all-start.2) | async-done | bytes 1769504 | tf_op jit(solution)/shard_map/all_to_all | solution.py:14
  98.9 1.1 copy.29
  100.0 1.3 copy.30
  101.4 6.8 %all-to-all-start.3 = ((bf16[16,3,144,128]{3,2,1,0:T(8,128)(2,1)}), bf16[16,3,144,128]{3,2,1,0:T(8,128)(2,1)S(1)}, u32[]{:S(2)}, u32[]{:S(2)}) async-start(bf16[16,3,144,128]{3,2,1,0:T(8,128)(2,1)} %copy.30), calls=%async_computation.3 | async-start | bytes 3538944 | tf_op jit(solution)/shard_map/all_to_all | solution.py:14
  108.2 1.7 %convert_reduce_fusion.1 = f32[3,144,128]{2,1,0:T(8,128)S(1)} fusion(bf16[16,3,144,128]{3,2,1,0:T(8,128)(2,1)} %all-to-all-done.2), kind=kLoop, calls=%fused_computation.4 | loop fusion | flops 1714176 | bytes 1990656 | tf_op jit(solution)/shard_map/reduce_sum | solution.py:29
  110.0 2.4 %collective-permute-start.2 = (f32[3,36,128]{2,1,0:T(8,128)S(1)}, f32[3,36,128]{2,1,0:T(8,128)S(1)}, u32[]{:S(2)}, u32[]{:S(2)}) collective-permute-start(f32[3,36,128]{2,1,0:T(8,128)S(1)} %get-tuple-element.17), channel_id=1, source_target_pairs={{0,3},{1,0},{2,1},{3,2},{4,7},{5,4},{6,5},{7,6},{8,11},{9,8},{10,9... | collective-permute-start | bytes 165896 | tf_op jit(solution)/shard_map/ppermute | solution.py:40
  113.0 1.2 collective-permute-done.2
  114.3 3.2 %collective-permute-done.1 = f32[3,36,128]{2,1,0:T(8,128)S(1)} collective-permute-done((f32[3,36,128]{2,1,0:T(8,128)S(1)}, f32[3,36,128]{2,1,0:T(8,128)S(1)}, u32[]{:S(2)}, u32[]{:S(2)}) %collective-permute-start.1) | collective-permute-done | bytes 55328 | tf_op jit(solution)/shard_map/ppermute | solution.py:40
  117.5 0.9 collective-permute-done
  118.4 4.5 %collective-permute-start.3 = (f32[3,36,128]{2,1,0:T(8,128)S(1)}, f32[3,36,128]{2,1,0:T(8,128)S(1)}, u32[]{:S(2)}, u32[]{:S(2)}) collective-permute-start(f32[3,36,128]{2,1,0:T(8,128)S(1)} %fusion.86), channel_id=1, source_target_pairs={{0,0},{16,64},{32,128},{48,192},{64,16},{80,80},{96,144},{112,208}... | collective-permute-start | bytes 165896 | tf_op jit(solution)/shard_map/ppermute | solution.py:84
  122.9 7.9 %collective-permute-done.3 = f32[3,36,128]{2,1,0:T(8,128)S(1)} collective-permute-done((f32[3,36,128]{2,1,0:T(8,128)S(1)}, f32[3,36,128]{2,1,0:T(8,128)S(1)}, u32[]{:S(2)}, u32[]{:S(2)}) %collective-permute-start.3) | collective-permute-done | bytes 55328 | tf_op jit(solution)/shard_map/ppermute | solution.py:84
  130.8 1.0 all-to-all-done.3
  132.8 3.6 %all-to-all-start.4 = ((f32[4,3,36,128]{3,2,1,0:T(8,128)}), f32[4,3,36,128]{3,2,1,0:T(8,128)S(1)}, u32[]{:S(2)}, u32[]{:S(2)}) async-start(f32[4,3,36,128]{3,2,1,0:T(8,128)} %copy.31), calls=%async_computation.4 | async-start | bytes 491520 | tf_op jit(solution)/shard_map/all_to_all | solution.py:14
  136.4 6.6 %all-to-all-done.4 = f32[4,3,36,128]{3,2,1,0:T(8,128)S(1)} async-done(((f32[4,3,36,128]{3,2,1,0:T(8,128)}), f32[4,3,36,128]{3,2,1,0:T(8,128)S(1)}, u32[]{:S(2)}, u32[]{:S(2)}) %all-to-all-start.4) | async-done | bytes 221216 | tf_op jit(solution)/shard_map/all_to_all | solution.py:14
  (55 shorter events, 10.1 us)
Async XLA Ops:
  14.6 7.6 %copy-start.10 = (f32[3,256]{1,0:T(4,128)S(1)}, f32[3,256]{1,0:T(4,128)}, u32[]{:S(2)}) copy-start(f32[3,256]{1,0:T(4,128)} %param.10) | copy-start | bytes 9220
  14.6 28.8 %all-to-all-start.1 = ((bf16[16,3,144,128]{3,2,1,0:T(8,128)(2,1)}), bf16[16,3,144,128]{3,2,1,0:T(8,128)(2,1)S(1)}, u32[]{:S(2)}, u32[]{:S(2)}) async-start(bf16[16,3,144,128]{3,2,1,0:T(8,128)(2,1)} %broadcast_in_dim.7), calls=%async_computation.1 | async-start | bytes 3538944 | tf_op jit(solution)/shard_map/all_to_all | solution.py:14
  43.4 2.6 %copy-start.11 = (bf16[3,2304,256]{2,1,0:T(8,128)(2,1)S(1)}, bf16[3,2304,256]{2,1,0:T(8,128)(2,1)}, u32[]{:S(2)}) copy-start(bf16[3,2304,256]{2,1,0:T(8,128)(2,1)} %param.9) | copy-start | bytes 10616836
  43.6 3.6 %copy-start.4 = (bf16[1,16,144,128]{3,2,0,1:T(8,128)(2,1)}, bf16[1,16,144,128]{3,2,0,1:T(8,128)(2,1)S(1)}, u32[]{:S(2)}) copy-start(bf16[1,16,144,128]{3,2,0,1:T(8,128)(2,1)S(1)} %get-tuple-element.15) | copy-start | bytes 1769476
  43.6 3.6 %copy-start.6 = (bf16[1,16,144,128]{3,2,0,1:T(8,128)(2,1)}, bf16[1,16,144,128]{3,2,0,1:T(8,128)(2,1)S(1)}, u32[]{:S(2)}) copy-start(bf16[1,16,144,128]{3,2,0,1:T(8,128)(2,1)S(1)} %get-tuple-element.14) | copy-start | bytes 1769476
  43.6 3.6 %copy-start.2 = (bf16[1,16,144,128]{3,2,0,1:T(8,128)(2,1)}, bf16[1,16,144,128]{3,2,0,1:T(8,128)(2,1)S(1)}, u32[]{:S(2)}) copy-start(bf16[1,16,144,128]{3,2,0,1:T(8,128)(2,1)S(1)} %get-tuple-element.13) | copy-start | bytes 1769476
  47.1 15.6 %copy-start.9 = (bf16[6,256,576]{1,2,0:T(8,128)(2,1)S(1)}, bf16[6,256,576]{1,2,0:T(8,128)(2,1)}, u32[]{:S(2)}) copy-start(bf16[6,256,576]{1,2,0:T(8,128)(2,1)} %param.11) | copy-start | bytes 5308420
  66.1 7.6 %copy-start.1 = (bf16[1,2,144,2304]{3,2,1,0:T(8,128)(2,1)S(1)}, bf16[1,2,144,2304]{3,2,1,0:T(8,128)(2,1)}, u32[]{:S(2)}) copy-start(bf16[1,2,144,2304]{3,2,1,0:T(8,128)(2,1)} %get-tuple-element.11) | copy-start | bytes 3981316
  66.1 7.6 %copy-start.7 = (bf16[1,16,144,128]{3,2,0,1:T(8,128)(2,1)S(1)}, bf16[1,16,144,128]{3,2,0,1:T(8,128)(2,1)}, u32[]{:S(2)}) copy-start(bf16[1,16,144,128]{3,2,0,1:T(8,128)(2,1)} %copy-done.6) | copy-start | bytes 1769476
  66.1 32.8 %all-to-all-start.2 = ((bf16[16,3,144,128]{3,2,1,0:T(8,128)(2,1)}), bf16[16,3,144,128]{3,2,1,0:T(8,128)(2,1)}, u32[]{:S(2)}, u32[]{:S(2)}) async-start(bf16[16,3,144,128]{3,2,1,0:T(8,128)(2,1)} %maximum_bitcast_fusion), calls=%async_computation.2 | async-start | bytes 3538944 | tf_op jit(solution)/shard_map/all_to_all | solution.py:14
  73.7 2.2 %copy-start = (bf16[1,2,144,2304]{3,2,1,0:T(8,128)(2,1)S(1)}, bf16[1,2,144,2304]{3,2,1,0:T(8,128)(2,1)}, u32[]{:S(2)}) copy-start(bf16[1,2,144,2304]{3,2,1,0:T(8,128)(2,1)} %get-tuple-element.12) | copy-start | bytes 3981316
  73.7 2.2 %copy-start.5 = (bf16[1,16,144,128]{3,2,0,1:T(8,128)(2,1)S(1)}, bf16[1,16,144,128]{3,2,0,1:T(8,128)(2,1)}, u32[]{:S(2)}) copy-start(bf16[1,16,144,128]{3,2,0,1:T(8,128)(2,1)} %copy-done.4) | copy-start | bytes 1769476
  74.3 2.2 %copy-start.8 = (bf16[3,144,2304]{2,1,0:T(8,128)(2,1)S(1)}, bf16[3,144,2304]{2,1,0:T(8,128)(2,1)}, u32[]{:S(2)}) copy-start(bf16[3,144,2304]{2,1,0:T(8,128)(2,1)} %param.8) | copy-start | bytes 5971972
  75.9 1.1 copy-start.3
  101.4 30.5 %all-to-all-start.3 = ((bf16[16,3,144,128]{3,2,1,0:T(8,128)(2,1)}), bf16[16,3,144,128]{3,2,1,0:T(8,128)(2,1)S(1)}, u32[]{:S(2)}, u32[]{:S(2)}) async-start(bf16[16,3,144,128]{3,2,1,0:T(8,128)(2,1)} %copy.30), calls=%async_computation.3 | async-start | bytes 3538944 | tf_op jit(solution)/shard_map/all_to_all | solution.py:14
  110.0 4.3 %collective-permute-start.2 = (f32[3,36,128]{2,1,0:T(8,128)S(1)}, f32[3,36,128]{2,1,0:T(8,128)S(1)}, u32[]{:S(2)}, u32[]{:S(2)}) collective-permute-start(f32[3,36,128]{2,1,0:T(8,128)S(1)} %get-tuple-element.17), channel_id=1, source_target_pairs={{0,3},{1,0},{2,1},{3,2},{4,7},{5,4},{6,5},{7,6},{8,11},{9,8},{10,9... | collective-permute-start | bytes 165896 | tf_op jit(solution)/shard_map/ppermute | solution.py:40
  112.4 5.1 %collective-permute-start.1 = (f32[3,36,128]{2,1,0:T(8,128)S(1)}, f32[3,36,128]{2,1,0:T(8,128)S(1)}, u32[]{:S(2)}, u32[]{:S(2)}) collective-permute-start(f32[3,36,128]{2,1,0:T(8,128)S(1)} %get-tuple-element.18), channel_id=1, source_target_pairs={{0,2},{1,3},{2,0},{3,1},{4,6},{5,7},{6,4},{7,5},{8,10},{9,11},{10,... | collective-permute-start | bytes 165896 | tf_op jit(solution)/shard_map/ppermute | solution.py:40
  112.4 6.0 %collective-permute-start = (f32[3,36,128]{2,1,0:T(8,128)S(1)}, f32[3,36,128]{2,1,0:T(8,128)S(1)}, u32[]{:S(2)}, u32[]{:S(2)}) collective-permute-start(f32[3,36,128]{2,1,0:T(8,128)S(1)} %get-tuple-element.16), channel_id=1, source_target_pairs={{0,1},{1,2},{2,3},{3,0},{4,5},{5,6},{6,7},{7,4},{8,9},{9,10},{10,1... | collective-permute-start | bytes 165896 | tf_op jit(solution)/shard_map/ppermute | solution.py:40
  118.4 12.4 %collective-permute-start.3 = (f32[3,36,128]{2,1,0:T(8,128)S(1)}, f32[3,36,128]{2,1,0:T(8,128)S(1)}, u32[]{:S(2)}, u32[]{:S(2)}) collective-permute-start(f32[3,36,128]{2,1,0:T(8,128)S(1)} %fusion.86), channel_id=1, source_target_pairs={{0,0},{16,64},{32,128},{48,192},{64,16},{80,80},{96,144},{112,208}... | collective-permute-start | bytes 165896 | tf_op jit(solution)/shard_map/ppermute | solution.py:84
  132.8 10.2 %all-to-all-start.4 = ((f32[4,3,36,128]{3,2,1,0:T(8,128)}), f32[4,3,36,128]{3,2,1,0:T(8,128)S(1)}, u32[]{:S(2)}, u32[]{:S(2)}) async-start(f32[4,3,36,128]{3,2,1,0:T(8,128)} %copy.31), calls=%async_computation.4 | async-start | bytes 491520 | tf_op jit(solution)/shard_map/all_to_all | solution.py:14

commit v3 on v1

v3 whole, which is shorter than its diff:
```python
import jax
import jax.numpy as jnp
from jax import lax
from jax.experimental import pallas as pl
from jax.experimental.pallas import tpu as pltpu
from jax.sharding import Mesh, PartitionSpec as P

BF16 = jnp.bfloat16
F32 = jnp.float32
ROWS = ("zh", "core")
PLANE = ("x", "y")
LAYERS = 3


def exchange(pieces, axis):
    return lax.all_to_all(pieces, axis, split_axis=0, concat_axis=0, tiled=True)


def from_everyone(shard, axis):
    count = lax.axis_size(axis)
    return exchange(jnp.broadcast_to(shard, (count, *shard.shape)), axis)


STEPS = (1, 3, 2)


def taken(array, index, dim):
    return lax.dynamic_index_in_dim(array, index, dim, False)


def passed_on(array, axis, step):
    count = lax.axis_size(axis)
    return lax.ppermute(array, axis, [(index, (index + step) % count) for index in range(count)])


def stepped(array, axis, step):
    count = lax.axis_size(axis)
    pairs = []
    for core in range(2):
        for index in range(count):
            pairs.append((core * count + index, core * count + (index + (step, count - step)[core]) % count))
    return lax.ppermute(array, ("core", axis), pairs)


def permuted_sums(arrays, axes, dims):
    places = [lax.axis_index(axis) for axis in axes]
    totals = [taken(array, place, dim).astype(F32) for array, place, dim in zip(arrays, places, dims)]
    for step in STEPS:
        for which, (array, axis, place, dim) in enumerate(zip(arrays, axes, places, dims)):
            count = array.shape[dim]
            onward = jnp.where(lax.axis_index("core") == 0, place + step, place + count - step) % count
            piece = stepped(taken(array, onward, dim), axis, step)
            totals[which] = totals[which] + piece.astype(F32)
    return totals


def encode_kernel(features, weight, bias, latent):
    layers, model, _ = weight.shape
    rows = features.shape[3]
    for layer in range(layers):
        rows_in = features[:, layer].reshape(model, rows)
        pre = lax.dot_general(rows_in, weight[layer], (((0,), (0,)), ((), ())), preferred_element_type=F32)
        latent[layer] = jnp.maximum(pre + bias[layer : layer + 1], 0.0).astype(BF16)


def encode(features, weight, bias):
    blocks, layers, deep, rows = features.shape
    _, model, wide = weight.shape
    return pl.pallas_call(
        encode_kernel,
        in_specs=[pl.BlockSpec(memory_space=pltpu.VMEM)] * 3,
        out_specs=pl.BlockSpec(memory_space=pltpu.VMEM),
        out_shape=jax.ShapeDtypeStruct((layers, rows, wide), BF16),
        cost_estimate=pl.CostEstimate(
            flops=2 * layers * model * wide * rows, bytes_accessed=2 * layers * model * (wide + rows), transcendentals=0
        ),
        name="encode",
    )(features, weight, bias)


def mlp_kernel(features, joined, down, out):
    layers, _, hidden, model = joined.shape
    rows = features.shape[3]
    for layer in range(layers):
        rows_in = features[:, layer].reshape(model, rows)
        pre = jnp.dot(joined[layer].reshape(2 * hidden, model), rows_in, preferred_element_type=F32)
        gate = pre[:hidden]
        cubic = gate + 0.044715 * (gate * gate * gate)
        act = 0.5 * gate * (1.0 + jnp.tanh(0.7978845608028654 * cubic)) * pre[hidden:]
        total = lax.dot_general(down[layer], act.astype(BF16), (((0,), (0,)), ((), ())), preferred_element_type=F32)
        out[layer] = total.reshape(out.shape[1:]).astype(BF16)


def mlp(features, joined, down):
    blocks, layers, deep, rows = features.shape
    _, _, hidden, model = joined.shape
    return pl.pallas_call(
        mlp_kernel,
        in_specs=[pl.BlockSpec(memory_space=pltpu.VMEM)] * 3,
        out_specs=pl.BlockSpec(memory_space=pltpu.VMEM),
        out_shape=jax.ShapeDtypeStruct((layers, blocks, deep, rows), BF16),
        cost_estimate=pl.CostEstimate(
            flops=6 * layers * model * hidden * rows,
            bytes_accessed=2 * layers * model * (3 * hidden + 2 * rows),
            transcendentals=layers * hidden * rows,
        ),
        name="mlp",
    )(features, joined, down)


def body(inputs, gate_up, down_weight, enc_weight, enc_bias, dec_weight):
    layers, rows, width = inputs.shape
    hidden = gate_up.shape[3]
    model = gate_up.shape[1]
    mine = jnp.swapaxes(inputs, 1, 2)
    decoder = jnp.swapaxes(dec_weight, 1, 2)
    beside = passed_on(decoder, "core", 1)
    second = lax.axis_index("core") == 1
    decoder = jnp.stack([jnp.where(second, beside, decoder), jnp.where(second, decoder, beside)])
    run = from_everyone(mine, "zl")
    run = jnp.moveaxis(run, 0, 1).reshape(layers, 4 * width, rows)
    everything = from_everyone(run, PLANE)
    everything, decoder = lax.optimization_barrier((everything, decoder))
    own = encode(everything, enc_weight, enc_bias)
    other = passed_on(own, "zh", 1)
    upper = lax.axis_index("zh") == 1
    both = jnp.stack([jnp.where(upper, other, own), jnp.where(upper, own, other)])

    everything, own = lax.optimization_barrier((everything, own))
    outs = mlp(everything, jnp.transpose(gate_up, (0, 2, 3, 1)), down_weight)
    recons = []
    for target in range(layers):
        total = None
        for source in range(target + 1):
            pair = target * (target + 1) // 2 + source
            term = jnp.einsum("cfk,rnk->rcfn", decoder[:, pair], both[:, source], preferred_element_type=F32)
            total = term if total is None else total + term
        recons.append(total.reshape(model, rows).astype(BF16))
    first = jnp.concatenate([jnp.stack(recons).reshape(outs.shape), outs]).reshape(2 * layers, 4, 4, 4 * width, rows)
    cut = 2 * width
    halves = permuted_sums([first[..., :cut, :], first[..., cut:, :]], ["x", "y"], [1, 2])
    halves = permuted_sums([half.astype(BF16) for half in halves], ["y", "x"], [1, 1])
    joint = jnp.concatenate(halves, axis=1).reshape(2 * layers, 4, width, rows)
    joint = permuted_sums([joint], ["zl"], [1])[0]
    summed = joint[:layers]
    swap = []
    for half in range(2):
        for place in range(4):
            swap.append((half * 4 + place, place // 2 * 4 + half * 2 + place % 2))
    recon = lax.ppermute(summed, ("zh", "x"), swap)
    residual = joint[layers:] - recon
    return jnp.swapaxes(recon, 1, 2), jnp.swapaxes(residual, 1, 2)


def solution(mesh):
    fine = Mesh(mesh.devices.reshape(2, 2, 4, 4, 4), ("zh", "core", "x", "y", "zl"))
    mp = ("x", "y", "zl")
    in_specs = (
        P(None, ROWS, mp),
        P(None, None, None, mp),
        P(None, mp, None),
        P(None, None, mp),
        P(None, mp),
        P(None, mp, ROWS),
    )
    out_specs = (P(None, ROWS, mp), P(None, ROWS, mp))
    return jax.shard_map(body, mesh=fine, in_specs=in_specs, out_specs=out_specs, check_vma=False)
```

time: 156 us -> 135 us (0.87)
  blocking collectives: 92.3 us -> 12 us
  starting transfers between devices: 13.6 us -> 48.6 us
  waiting for transfers between devices: 23.9 us -> 42 us
  Pallas kernels: 0 us -> 12.3 us
  matrix products: 11.7 us -> 2.07 us
  other arithmetic: 1.22 us -> 8.95 us
  local copies, waits for them, and re-layouts: 12.2 us -> 7.52 us
    all_to_all x3 -> x1, blocking collectives: 77.3 us -> 12 us  [exchange(): return lax.all_to_all(pieces, axis, split_axis=0, concat_axis=0, tiled=True)]
    ppermute x1 -> x18, starting transfers between devices: 6.04 us -> 41 us  [the longest x15 29 us: stepped(): return lax.ppermute(array, ('core', axis), pairs)]
    ppermute x1 -> x18, waiting for transfers between devices: 6.51 us -> 23.6 us  [the longest x15 18.5 us: stepped(): return lax.ppermute(array, ('core', axis), pairs)]
    all_gather x1 -> x0, blocking collectives: 15.1 us -> none  [body(): gathered = lax.all_gather(jnp.stack(latents), ROWS, axis=0)]
    pallas_call x0 -> x2, Pallas kernels: none -> 12.3 us  [the longest x1 8.34 us: mlp(): pl.pallas_call(mlp_kernel, in_specs=[pl.BlockSpec(memory_space=pltpu.VMEM...]
    dot_general x15 -> x6, matrix products: 11.7 us -> 2.07 us  [body(): jnp.einsum('cfk,rnk->rcfn', decoder[:, pair], both[:, source], preferred_...]
    another operation x1 -> x3, other arithmetic: 0.03 us -> 4.83 us  [the longest x2 3.78 us: body(): jnp.stack([jnp.where(second, beside, decoder), jnp.where(second, decoder,...]
    slice x4 -> x2, local copies, waits for them, and re-layouts: 4 us -> 0.83 us  [the longest x1 0.83 us: body(): first[..., :cut, :]]
  transfers between devices with their start and end apart: 2 -> 19, of which waited for: 2 -> 9; matrix products, arithmetic and copies ran while one was open for 2% -> 7% of each run, Pallas kernels for 0% -> 6%
where the time goes in v3:
time: 135 us; the launch traced here: 134 us
  starting transfers between devices  48.6 us (36%)
  waiting for transfers between devices  42 us (31%)
  Pallas kernels  12.3 us (9%)
  blocking collectives  12 us (9%)
  other arithmetic  8.95 us (7%)
  local copies, waits for them, and re-layouts  7.52 us (6%)
  matrix products  2.07 us (2%)
    ppermute x15, starting transfers between devices, stepped(): return lax.ppermute(array, ('core', axis), pairs)  29 us
    ppermute x15, waiting for transfers between devices, stepped(): return lax.ppermute(array, ('core', axis), pairs)  18.5 us
    all_to_all x1, waiting for transfers between devices, exchange(): return lax.all_to_all(pieces, axis, split_axis=0, concat_axis=0, tiled=True)  18.4 us
    all_to_all x1, blocking collectives, exchange(): return lax.all_to_all(pieces, axis, split_axis=0, concat_axis=0, tiled=True)  12 us
    pallas_call x1, Pallas kernels, mlp(): pl.pallas_call(mlp_kernel, in_specs=[pl.BlockSpec(memory_space=pltpu.VMEM...  8.34 us
    all_to_all x1, starting transfers between devices, exchange(): return lax.all_to_all(pieces, axis, split_axis=0, concat_axis=0, tiled=True)  7.58 us
    ppermute x1, starting transfers between devices, body(): recon = lax.ppermute(summed, ('zh', 'x'), swap)  7.36 us
    ppermute x1, waiting for transfers between devices, body(): recon = lax.ppermute(summed, ('zh', 'x'), swap)  5.06 us
  transfers between devices with their start and end apart: 19, of which 9 were waited for; matrix products, arithmetic and copies ran while one was open for 7% of the time, Pallas kernels for 6%

profile of v3, /device:TPU:4, one launch (start us, length us, event | category | flops | bytes accessed | tf_op | source)
XLA Modules:
  0.0 134.3 jit_solution(4096974059726873913)
XLA Ops:
  1.5 12.0 %all_to_all.10 = bf16[4,3,36,128]{3,2,1,0:T(8,128)(2,1)S(1)} all-to-all(bf16[4,3,36,128]{3,2,1,0:T(8,128)(2,1)S(1)} %broadcast_in_dim.6), channel_id=1, replica_groups=mesh['zh'=2,'core'=2,'x'=4,'y'=4,'zl'=4] {'zl'}, dimensions={0} | all-to-all | bytes 221184 | tf_op jit(solution)/shard_map/all_to_all | solution.py:16
  13.6 1.5 %broadcast_in_dim.7 = bf16[16,3,144,128]{3,2,1,0:T(8,128)(2,1)} broadcast(bf16[3,144,128]{2,1,0:T(8,128)(2,1)S(1)} %reshape.69), dimensions={1,2,3} | broadcast | bytes 1880064 | tf_op jit(solution)/shard_map/broadcast_in_dim | solution.py:21
  15.0 7.6 %all-to-all-start.1 = ((bf16[16,3,144,128]{3,2,1,0:T(8,128)(2,1)}), bf16[16,3,144,128]{3,2,1,0:T(8,128)(2,1)S(1)}, u32[]{:S(2)}, u32[]{:S(2)}) async-start(bf16[16,3,144,128]{3,2,1,0:T(8,128)(2,1)} %broadcast_in_dim.7), calls=%async_computation.1 | async-start | bytes 3538944 | tf_op jit(solution)/shard_map/all_to_all | solution.py:16
  22.6 1.7 %select_bitcast_fusion.1 = (bf16[1,6,576,256]{3,2,0,1:T(8,128)(2,1)S(1)}, bf16[1,6,576,256]{3,2,0,1:T(8,128)(2,1)S(1)}) fusion(bf16[6,576,256]{2,1,0:T(8,128)(2,1)} %collective-permute-done, pred[]{:T(512)S(6)} %eq.40, bf16[6,256,576]{1,2,0:T(8,128)(2,1)S(1)} %copy-done.3), kind=kLoop, calls=%fused_computation.3 | loop fusion | flops 1769472 | bytes 7077889 | tf_op jit(solution)/shard_map/stack | solution.py:119
  24.4 2.1 %pad_maximum_fusion = bf16[2,6,576,256]{3,2,0,1:T(8,128)(2,1)} fusion(bf16[1,6,576,256]{3,2,0,1:T(8,128)(2,1)S(1)} %get-tuple-element.11, bf16[1,6,576,256]{3,2,0,1:T(8,128)(2,1)S(1)} %get-tuple-element.10), kind=kLoop, calls=%fused_computation | loop fusion | flops 1769472 | bytes 7077888 | tf_op jit(solution)/shard_map/stack | solution.py:119
  26.4 18.4 %all-to-all-done.1.features = bf16[16,3,144,128]{3,2,1,0:T(8,128)(2,1)S(1)} async-done(((bf16[16,3,144,128]{3,2,1,0:T(8,128)(2,1)}), bf16[16,3,144,128]{3,2,1,0:T(8,128)(2,1)S(1)}, u32[]{:S(2)}, u32[]{:S(2)}) %all-to-all-start.1) | async-done | bytes 1769504 | tf_op jit(solution)/shard_map/all_to_all | solution.py:16
  46.1 3.9 %encode.1 = bf16[3,128,256]{2,1,0:T(8,128)(2,1)} custom-call(bf16[16,3,144,128]{3,2,1,0:T(8,128)(2,1)} %copy-done, bf16[3,2304,256]{2,1,0:T(8,128)(2,1)} %weight.1, f32[3,256]{1,0:T(4,128)} %bias.1), custom_call_target="tpu_custom_call" | custom-call | flops 452984832 | bytes 5308416 | tf_op jit(solution)/shard_map/encode/pallas_call | solution.py:69
  50.0 4.5 %collective-permute-start.1 = (bf16[3,128,256]{2,1,0:T(8,128)(2,1)}, bf16[3,128,256]{2,1,0:T(8,128)(2,1)}, u32[]{:S(2)}, u32[]{:S(2)}) collective-permute-start(bf16[3,128,256]{2,1,0:T(8,128)(2,1)} %encode.1), channel_id=1, source_target_pairs={{0,128},{128,0},{1,129},{129,1},{2,130},{130,2},{3,131},{131,3},{4... | collective-permute-start | bytes 589832 | tf_op jit(solution)/shard_map/ppermute | solution.py:33
  54.5 8.3 %mlp.1 = bf16[3,16,144,128]{3,2,1,0:T(8,128)(2,1)} custom-call(bf16[16,3,144,128]{3,2,1,0:T(8,128)(2,1)} %copy-done, bf16[3,2,144,2304]{3,2,1,0:T(8,128)(2,1)} %bitcast.133, bf16[3,144,2304]{2,1,0:T(8,128)(2,1)} %down.1), custom_call_target="tpu_custom_call" | custom-call | flops 764411904 | bytes 9510912 | tf_op jit(solution)/shard_map/mlp/pallas_call | solution.py:97
  69.4 1.9 %collective-permute-start.2 = (bf16[6,4,72,128]{3,2,0,1:T(8,128)(2,1)}, bf16[6,4,72,128]{3,2,0,1:T(8,128)(2,1)}, u32[]{:S(2)}, u32[]{:S(2)}) collective-permute-start(bf16[6,4,72,128]{3,2,0,1:T(8,128)(2,1)} %bitcast.131), channel_id=1, source_target_pairs={{0,16},{16,32},{32,48},{48,0},{64,112},{80,64},{96,80},{112,96},{1... | collective-permute-start | bytes 1327112 | tf_op jit(solution)/shard_map/ppermute | solution.py:42
  71.5 4.1 %collective-permute-start.4 = (bf16[6,4,72,128]{3,2,0,1:T(8,128)(2,1)S(1)}, bf16[6,4,72,128]{3,2,0,1:T(8,128)(2,1)}, u32[]{:S(2)}, u32[]{:S(2)}) collective-permute-start(bf16[6,4,72,128]{3,2,0,1:T(8,128)(2,1)S(1)} %bitcast.140), channel_id=1, source_target_pairs={{0,32},{16,48},{32,0},{48,16},{64,96},{80,112},{96,64},{112,80},{1... | collective-permute-start | bytes 1327112 | tf_op jit(solution)/shard_map/ppermute | solution.py:42
  76.6 5.2 %collective-permute-done.2 = bf16[6,4,72,128]{3,2,0,1:T(8,128)(2,1)} collective-permute-done((bf16[6,4,72,128]{3,2,0,1:T(8,128)(2,1)}, bf16[6,4,72,128]{3,2,0,1:T(8,128)(2,1)}, u32[]{:S(2)}, u32[]{:S(2)}) %collective-permute-start.2) | collective-permute-done | bytes 442400 | tf_op jit(solution)/shard_map/ppermute | solution.py:42
  81.8 9.7 %collective-permute-start.9 = (bf16[6,4,72,128]{3,2,0,1:T(8,128)(2,1)S(1)}, bf16[6,4,72,128]{3,2,0,1:T(8,128)(2,1)}, u32[]{:S(2)}, u32[]{:S(2)}) collective-permute-start(bf16[6,4,72,128]{3,2,0,1:T(8,128)(2,1)S(1)} %bitcast.142), channel_id=1, source_target_pairs={{0,12},{4,0},{8,4},{12,8},{64,68},{68,72},{72,76},{76,64},{1,13},{... | collective-permute-start | bytes 1327112 | tf_op jit(solution)/shard_map/ppermute | solution.py:42
  91.6 1.5 %fusion.7 = bf16[6,4,72,128]{3,2,0,1:T(8,128)(2,1)S(1)} fusion(bf16[6,4,72,128]{3,2,0,1:T(8,128)(2,1)} %collective-permute-done.4, bf16[6,4,72,128]{3,2,0,1:T(8,128)(2,1)} %collective-permute-done.3, bf16[6,4,72,128]{3,2,0,1:T(8,128)(2,1)} %collective-permute-done.2, bf16[6,1,4,72,128]{4,3,2,1,0:T(8,128)(2,1)S(1)} %get-tuple-element.12), kind=kLoop, calls=%fused_computation.17 | loop fusion | flops 1769472 | bytes 2211840 | tf_op jit(solution)/shard_map/convert_element_type | solution.py:142
  93.2 3.2 %collective-permute-start.6 = (bf16[6,72,128]{2,1,0:T(8,128)(2,1)S(1)}, bf16[6,72,128]{2,1,0:T(8,128)(2,1)S(1)}, u32[]{:S(2)}, u32[]{:S(2)}) collective-permute-start(bf16[6,72,128]{2,1,0:T(8,128)(2,1)S(1)} %get-tuple-element.25), channel_id=1, source_target_pairs={{0,12},{4,0},{8,4},{12,8},{64,68},{68,72},{72,76},{76,64},{1,13},{... | collective-permute-start | bytes 331784 | tf_op jit(solution)/shard_map/ppermute | solution.py:42
  96.5 3.3 %collective-permute-done.9 = bf16[6,4,72,128]{3,2,0,1:T(8,128)(2,1)} collective-permute-done((bf16[6,4,72,128]{3,2,0,1:T(8,128)(2,1)S(1)}, bf16[6,4,72,128]{3,2,0,1:T(8,128)(2,1)}, u32[]{:S(2)}, u32[]{:S(2)}) %collective-permute-start.9) | collective-permute-done | bytes 442400 | tf_op jit(solution)/shard_map/ppermute | solution.py:42
  101.3 2.0 %collective-permute-start.12 = (bf16[6,72,128]{2,1,0:T(8,128)(2,1)S(1)}, bf16[6,72,128]{2,1,0:T(8,128)(2,1)S(1)}, u32[]{:S(2)}, u32[]{:S(2)}) collective-permute-start(bf16[6,72,128]{2,1,0:T(8,128)(2,1)S(1)} %get-tuple-element.28), channel_id=1, source_target_pairs={{0,48},{16,0},{32,16},{48,32},{64,80},{80,96},{96,112},{112,64},{1... | collective-permute-start | bytes 331784 | tf_op jit(solution)/shard_map/ppermute | solution.py:42
  103.3 3.1 %collective-permute-start.13 = (bf16[6,72,128]{2,1,0:T(8,128)(2,1)S(1)}, bf16[6,72,128]{2,1,0:T(8,128)(2,1)S(1)}, u32[]{:S(2)}, u32[]{:S(2)}) collective-permute-start(bf16[6,72,128]{2,1,0:T(8,128)(2,1)S(1)} %get-tuple-element.27), channel_id=1, source_target_pairs={{0,32},{16,48},{32,0},{48,16},{64,96},{80,112},{96,64},{112,80},{1... | collective-permute-start | bytes 331784 | tf_op jit(solution)/shard_map/ppermute | solution.py:42
  107.0 2.5 %collective-permute-done.13 = bf16[6,72,128]{2,1,0:T(8,128)(2,1)S(1)} collective-permute-done((bf16[6,72,128]{2,1,0:T(8,128)(2,1)S(1)}, bf16[6,72,128]{2,1,0:T(8,128)(2,1)S(1)}, u32[]{:S(2)}, u32[]{:S(2)}) %collective-permute-start.13) | collective-permute-done | bytes 110624 | tf_op jit(solution)/shard_map/ppermute | solution.py:42
  111.2 2.5 %collective-permute-start.15 = (f32[6,36,128]{2,1,0:T(8,128)S(1)}, f32[6,36,128]{2,1,0:T(8,128)S(1)}, u32[]{:S(2)}, u32[]{:S(2)}) collective-permute-start(f32[6,36,128]{2,1,0:T(8,128)S(1)} %get-tuple-element.22), channel_id=1, source_target_pairs={{0,3},{1,0},{2,1},{3,2},{64,65},{65,66},{66,67},{67,64},{4,7},{5,4... | collective-permute-start | bytes 331784 | tf_op jit(solution)/shard_map/ppermute | solution.py:42
  113.7 3.0 %collective-permute-done.14 = f32[6,36,128]{2,1,0:T(8,128)S(1)} collective-permute-done((f32[6,36,128]{2,1,0:T(8,128)S(1)}, f32[6,36,128]{2,1,0:T(8,128)S(1)}, u32[]{:S(2)}, u32[]{:S(2)}) %collective-permute-start.14) | collective-permute-done | bytes 110624 | tf_op jit(solution)/shard_map/ppermute | solution.py:42
  117.4 3.1 %collective-permute-done.16 = f32[6,36,128]{2,1,0:T(8,128)S(1)} collective-permute-done((f32[6,36,128]{2,1,0:T(8,128)S(1)}, f32[6,36,128]{2,1,0:T(8,128)S(1)}, u32[]{:S(2)}, u32[]{:S(2)}) %collective-permute-start.16) | collective-permute-done | bytes 110624 | tf_op jit(solution)/shard_map/ppermute | solution.py:42
  120.6 7.4 %collective-permute-start.17 = (f32[3,36,128]{2,1,0:T(8,128)S(1)}, f32[3,36,128]{2,1,0:T(8,128)S(1)}, u32[]{:S(2)}, u32[]{:S(2)}) collective-permute-start(f32[3,36,128]{2,1,0:T(8,128)S(1)} %slice.61), channel_id=1, source_target_pairs={{0,0},{16,16},{32,128},{48,144},{128,32},{144,48},{160,160},{176,1... | collective-permute-start | bytes 165896 | tf_op jit(solution)/shard_map/ppermute | solution.py:150
  127.9 5.1 %collective-permute-done.17 = f32[3,36,128]{2,1,0:T(8,128)S(1)} collective-permute-done((f32[3,36,128]{2,1,0:T(8,128)S(1)}, f32[3,36,128]{2,1,0:T(8,128)S(1)}, u32[]{:S(2)}, u32[]{:S(2)}) %collective-permute-start.17) | collective-permute-done | bytes 55328 | tf_op jit(solution)/shard_map/ppermute | solution.py:150
  (61 shorter events, 15.8 us)
Async XLA Ops:
  0.6 22.0 %collective-permute-start = (bf16[6,576,256]{2,1,0:T(8,128)(2,1)}, bf16[6,576,256]{2,1,0:T(8,128)(2,1)}, u32[]{:S(2)}, u32[]{:S(2)}) collective-permute-start(bf16[6,576,256]{2,1,0:T(8,128)(2,1)} %bitcast.137), channel_id=1, source_target_pairs={{0,64},{64,0},{1,65},{65,1},{2,66},{66,2},{3,67},{67,3},{4,68},{68... | collective-permute-start | bytes 5308424 | tf_op jit(solution)/shard_map/ppermute | solution.py:33
  15.0 7.6 %copy-start.3 = (bf16[6,256,576]{1,2,0:T(8,128)(2,1)S(1)}, bf16[6,256,576]{1,2,0:T(8,128)(2,1)}, u32[]{:S(2)}) copy-start(bf16[6,256,576]{1,2,0:T(8,128)(2,1)} %param.11) | copy-start | bytes 5308420
  15.0 29.8 %all-to-all-start.1 = ((bf16[16,3,144,128]{3,2,1,0:T(8,128)(2,1)}), bf16[16,3,144,128]{3,2,1,0:T(8,128)(2,1)S(1)}, u32[]{:S(2)}, u32[]{:S(2)}) async-start(bf16[16,3,144,128]{3,2,1,0:T(8,128)(2,1)} %broadcast_in_dim.7), calls=%async_computation.1 | async-start | bytes 3538944 | tf_op jit(solution)/shard_map/all_to_all | solution.py:16
  44.9 1.2 copy-start
  50.0 12.8 %collective-permute-start.1 = (bf16[3,128,256]{2,1,0:T(8,128)(2,1)}, bf16[3,128,256]{2,1,0:T(8,128)(2,1)}, u32[]{:S(2)}, u32[]{:S(2)}) collective-permute-start(bf16[3,128,256]{2,1,0:T(8,128)(2,1)} %encode.1), channel_id=1, source_target_pairs={{0,128},{128,0},{1,129},{129,1},{2,130},{130,2},{3,131},{131,3},{4... | collective-permute-start | bytes 589832 | tf_op jit(solution)/shard_map/ppermute | solution.py:33
  54.5 9.4 %copy-start.1 = (bf16[2,6,576,256]{3,2,0,1:T(8,128)(2,1)S(1)}, bf16[2,6,576,256]{3,2,0,1:T(8,128)(2,1)}, u32[]{:S(2)}) copy-start(bf16[2,6,576,256]{3,2,0,1:T(8,128)(2,1)} %pad_maximum_fusion) | copy-start | bytes 10616836
  65.7 1.5 %copy-start.2 = (bf16[3,16,144,128]{3,2,1,0:T(8,128)(2,1)S(1)}, bf16[3,16,144,128]{3,2,1,0:T(8,128)(2,1)}, u32[]{:S(2)}) copy-start(bf16[3,16,144,128]{3,2,1,0:T(8,128)(2,1)} %mlp.1) | copy-start | bytes 5308420
  69.4 12.5 %collective-permute-start.2 = (bf16[6,4,72,128]{3,2,0,1:T(8,128)(2,1)}, bf16[6,4,72,128]{3,2,0,1:T(8,128)(2,1)}, u32[]{:S(2)}, u32[]{:S(2)}) collective-permute-start(bf16[6,4,72,128]{3,2,0,1:T(8,128)(2,1)} %bitcast.131), channel_id=1, source_target_pairs={{0,16},{16,32},{32,48},{48,0},{64,112},{80,64},{96,80},{112,96},{1... | collective-permute-start | bytes 1327112 | tf_op jit(solution)/shard_map/ppermute | solution.py:42
  71.3 20.3 %collective-permute-start.3 = (bf16[6,4,72,128]{3,2,0,1:T(8,128)(2,1)S(1)}, bf16[6,4,72,128]{3,2,0,1:T(8,128)(2,1)}, u32[]{:S(2)}, u32[]{:S(2)}) collective-permute-start(bf16[6,4,72,128]{3,2,0,1:T(8,128)(2,1)S(1)} %bitcast.139), channel_id=1, source_target_pairs={{0,48},{16,0},{32,16},{48,32},{64,80},{80,96},{96,112},{112,64},{1... | collective-permute-start | bytes 1327112 | tf_op jit(solution)/shard_map/ppermute | solution.py:42
  71.5 20.0 %collective-permute-start.4 = (bf16[6,4,72,128]{3,2,0,1:T(8,128)(2,1)S(1)}, bf16[6,4,72,128]{3,2,0,1:T(8,128)(2,1)}, u32[]{:S(2)}, u32[]{:S(2)}) collective-permute-start(bf16[6,4,72,128]{3,2,0,1:T(8,128)(2,1)S(1)} %bitcast.140), channel_id=1, source_target_pairs={{0,32},{16,48},{32,0},{48,16},{64,96},{80,112},{96,64},{112,80},{1... | collective-permute-start | bytes 1327112 | tf_op jit(solution)/shard_map/ppermute | solution.py:42
  75.8 20.6 %collective-permute-start.10 = (bf16[6,4,72,128]{3,2,0,1:T(8,128)(2,1)S(1)}, bf16[6,4,72,128]{3,2,0,1:T(8,128)(2,1)S(1)}, u32[]{:S(2)}, u32[]{:S(2)}) collective-permute-start(bf16[6,4,72,128]{3,2,0,1:T(8,128)(2,1)S(1)} %bitcast.143), channel_id=1, source_target_pairs={{0,8},{4,12},{8,0},{12,4},{64,72},{68,76},{72,64},{76,68},{1,9},{5... | collective-permute-start | bytes 1327112 | tf_op jit(solution)/shard_map/ppermute | solution.py:42
  76.3 20.1 %collective-permute-start.8 = (bf16[6,4,72,128]{3,2,0,1:T(8,128)(2,1)S(1)}, bf16[6,4,72,128]{3,2,0,1:T(8,128)(2,1)}, u32[]{:S(2)}, u32[]{:S(2)}) collective-permute-start(bf16[6,4,72,128]{3,2,0,1:T(8,128)(2,1)S(1)} %bitcast.141), channel_id=1, source_target_pairs={{0,4},{4,8},{8,12},{12,0},{64,76},{68,64},{72,68},{76,72},{1,5},{5... | collective-permute-start | bytes 1327112 | tf_op jit(solution)/shard_map/ppermute | solution.py:42
  81.8 18.0 %collective-permute-start.9 = (bf16[6,4,72,128]{3,2,0,1:T(8,128)(2,1)S(1)}, bf16[6,4,72,128]{3,2,0,1:T(8,128)(2,1)}, u32[]{:S(2)}, u32[]{:S(2)}) collective-permute-start(bf16[6,4,72,128]{3,2,0,1:T(8,128)(2,1)S(1)} %bitcast.142), channel_id=1, source_target_pairs={{0,12},{4,0},{8,4},{12,8},{64,68},{68,72},{72,76},{76,64},{1,13},{... | collective-permute-start | bytes 1327112 | tf_op jit(solution)/shard_map/ppermute | solution.py:42
  93.1 10.2 %collective-permute-start.5 = (bf16[6,72,128]{2,1,0:T(8,128)(2,1)S(1)}, bf16[6,72,128]{2,1,0:T(8,128)(2,1)S(1)}, u32[]{:S(2)}, u32[]{:S(2)}) collective-permute-start(bf16[6,72,128]{2,1,0:T(8,128)(2,1)S(1)} %get-tuple-element.23), channel_id=1, source_target_pairs={{0,4},{4,8},{8,12},{12,0},{64,76},{68,64},{72,68},{76,72},{1,5},{5... | collective-permute-start | bytes 331784 | tf_op jit(solution)/shard_map/ppermute | solution.py:42
  93.2 13.2 %collective-permute-start.6 = (bf16[6,72,128]{2,1,0:T(8,128)(2,1)S(1)}, bf16[6,72,128]{2,1,0:T(8,128)(2,1)S(1)}, u32[]{:S(2)}, u32[]{:S(2)}) collective-permute-start(bf16[6,72,128]{2,1,0:T(8,128)(2,1)S(1)} %get-tuple-element.25), channel_id=1, source_target_pairs={{0,12},{4,0},{8,4},{12,8},{64,68},{68,72},{72,76},{76,64},{1,13},{... | collective-permute-start | bytes 331784 | tf_op jit(solution)/shard_map/ppermute | solution.py:42
  96.4 9.9 %collective-permute-start.7 = (bf16[6,72,128]{2,1,0:T(8,128)(2,1)S(1)}, bf16[6,72,128]{2,1,0:T(8,128)(2,1)S(1)}, u32[]{:S(2)}, u32[]{:S(2)}) collective-permute-start(bf16[6,72,128]{2,1,0:T(8,128)(2,1)S(1)} %get-tuple-element.24), channel_id=1, source_target_pairs={{0,8},{4,12},{8,0},{12,4},{64,72},{68,76},{72,64},{76,68},{1,9},{5... | collective-permute-start | bytes 331784 | tf_op jit(solution)/shard_map/ppermute | solution.py:42
  101.2 5.3 %collective-permute-start.11 = (bf16[6,72,128]{2,1,0:T(8,128)(2,1)S(1)}, bf16[6,72,128]{2,1,0:T(8,128)(2,1)S(1)}, u32[]{:S(2)}, u32[]{:S(2)}) collective-permute-start(bf16[6,72,128]{2,1,0:T(8,128)(2,1)S(1)} %get-tuple-element.26), channel_id=1, source_target_pairs={{0,16},{16,32},{32,48},{48,0},{64,112},{80,64},{96,80},{112,96},{1... | collective-permute-start | bytes 331784 | tf_op jit(solution)/shard_map/ppermute | solution.py:42
  101.3 5.7 %collective-permute-start.12 = (bf16[6,72,128]{2,1,0:T(8,128)(2,1)S(1)}, bf16[6,72,128]{2,1,0:T(8,128)(2,1)S(1)}, u32[]{:S(2)}, u32[]{:S(2)}) collective-permute-start(bf16[6,72,128]{2,1,0:T(8,128)(2,1)S(1)} %get-tuple-element.28), channel_id=1, source_target_pairs={{0,48},{16,0},{32,16},{48,32},{64,80},{80,96},{96,112},{112,64},{1... | collective-permute-start | bytes 331784 | tf_op jit(solution)/shard_map/ppermute | solution.py:42
  103.3 6.3 %collective-permute-start.13 = (bf16[6,72,128]{2,1,0:T(8,128)(2,1)S(1)}, bf16[6,72,128]{2,1,0:T(8,128)(2,1)S(1)}, u32[]{:S(2)}, u32[]{:S(2)}) collective-permute-start(bf16[6,72,128]{2,1,0:T(8,128)(2,1)S(1)} %get-tuple-element.27), channel_id=1, source_target_pairs={{0,32},{16,48},{32,0},{48,16},{64,96},{80,112},{96,64},{112,80},{1... | collective-permute-start | bytes 331784 | tf_op jit(solution)/shard_map/ppermute | solution.py:42
  109.8 6.9 %collective-permute-start.14 = (f32[6,36,128]{2,1,0:T(8,128)S(1)}, f32[6,36,128]{2,1,0:T(8,128)S(1)}, u32[]{:S(2)}, u32[]{:S(2)}) collective-permute-start(f32[6,36,128]{2,1,0:T(8,128)S(1)} %get-tuple-element.20), channel_id=1, source_target_pairs={{0,1},{1,2},{2,3},{3,0},{64,67},{65,64},{66,65},{67,66},{4,5},{5,6... | collective-permute-start | bytes 331784 | tf_op jit(solution)/shard_map/ppermute | solution.py:42
  111.2 6.2 %collective-permute-start.15 = (f32[6,36,128]{2,1,0:T(8,128)S(1)}, f32[6,36,128]{2,1,0:T(8,128)S(1)}, u32[]{:S(2)}, u32[]{:S(2)}) collective-permute-start(f32[6,36,128]{2,1,0:T(8,128)S(1)} %get-tuple-element.22), channel_id=1, source_target_pairs={{0,3},{1,0},{2,1},{3,2},{64,65},{65,66},{66,67},{67,64},{4,7},{5,4... | collective-permute-start | bytes 331784 | tf_op jit(solution)/shard_map/ppermute | solution.py:42
  113.7 6.8 %collective-permute-start.16 = (f32[6,36,128]{2,1,0:T(8,128)S(1)}, f32[6,36,128]{2,1,0:T(8,128)S(1)}, u32[]{:S(2)}, u32[]{:S(2)}) collective-permute-start(f32[6,36,128]{2,1,0:T(8,128)S(1)} %get-tuple-element.21), channel_id=1, source_target_pairs={{0,2},{1,3},{2,0},{3,1},{64,66},{65,67},{66,64},{67,65},{4,6},{5,7... | collective-permute-start | bytes 331784 | tf_op jit(solution)/shard_map/ppermute | solution.py:42
  120.6 12.4 %collective-permute-start.17 = (f32[3,36,128]{2,1,0:T(8,128)S(1)}, f32[3,36,128]{2,1,0:T(8,128)S(1)}, u32[]{:S(2)}, u32[]{:S(2)}) collective-permute-start(f32[3,36,128]{2,1,0:T(8,128)S(1)} %slice.61), channel_id=1, source_target_pairs={{0,0},{16,16},{32,128},{48,144},{128,32},{144,48},{160,160},{176,1... | collective-permute-start | bytes 165896 | tf_op jit(solution)/shard_map/ppermute | solution.py:150

commit v4 on v3

--- a/solution.py
+++ b/solution.py
@@ -54,6 +54,25 @@
     return totals
 
 
+def fetch_kernel(source, kept, arrived):
+    copy = pltpu.make_async_copy(source, kept, arrived)
+    copy.start()
+    copy.wait()
+
+
+def fetch(weight):
+    return pl.pallas_call(
+        fetch_kernel,
+        in_specs=[pl.BlockSpec(memory_space=pl.ANY)],
+        out_specs=pl.BlockSpec(memory_space=pltpu.VMEM),
+        out_shape=jax.ShapeDtypeStruct(weight.shape, weight.dtype),
+        scratch_shapes=[pltpu.SemaphoreType.DMA],
+        cost_estimate=pl.CostEstimate(flops=0, bytes_accessed=4 * weight.size, transcendentals=0),
+        compiler_params=pltpu.CompilerParams(vmem_limit_bytes=6 << 20),
+        name="fetch",
+    )(weight)
+
+
 def encode_kernel(features, weight, bias, latent):
     layers, model, _ = weight.shape
     rows = features.shape[3]
@@ -74,6 +93,7 @@
         cost_estimate=pl.CostEstimate(
             flops=2 * layers * model * wide * rows, bytes_accessed=2 * layers * model * (wide + rows), transcendentals=0
         ),
+        compiler_params=pltpu.CompilerParams(vmem_limit_bytes=8 << 20),
         name="encode",
     )(features, weight, bias)
 
@@ -104,6 +124,7 @@
             bytes_accessed=2 * layers * model * (3 * hidden + 2 * rows),
             transcendentals=layers * hidden * rows,
         ),
+        compiler_params=pltpu.CompilerParams(vmem_limit_bytes=16 << 20),
         name="mlp",
     )(features, joined, down)
 
@@ -120,8 +141,8 @@
     run = from_everyone(mine, "zl")
     run = jnp.moveaxis(run, 0, 1).reshape(layers, 4 * width, rows)
     everything = from_everyone(run, PLANE)
-    everything, decoder = lax.optimization_barrier((everything, decoder))
-    own = encode(everything, enc_weight, enc_bias)
+    everything, decoder, encoder = lax.optimization_barrier((everything, decoder, fetch(enc_weight)))
+    own = encode(everything, encoder, enc_bias)
     other = passed_on(own, "zh", 1)
     upper = lax.axis_index("zh") == 1
     both = jnp.stack([jnp.where(upper, other, own), jnp.where(upper, own, other)])

time: 135 us -> 129 us (0.956); the launches traced: 134 us -> 126 us
  Pallas kernels: 12.3 us -> 4.79 us
  local copies, waits for them, and re-layouts: 7.52 us -> 14.6 us
  starting transfers between devices: 48.6 us -> 41.6 us
    ppermute x15, starting transfers between devices: 29 us -> 21.6 us  [stepped(): return lax.ppermute(array, ('core', axis), pairs)]
    unnamed x15 -> x23, local copies, waits for them, and re-layouts: 3.95 us -> 11 us
    ppermute x15, waiting for transfers between devices: 18.5 us -> 23.3 us  [stepped(): return lax.ppermute(array, ('core', axis), pairs)]
    pallas_call x1, Pallas kernels: 8.34 us -> 3.68 us  [mlp(): pl.pallas_call(mlp_kernel, in_specs=[pl.BlockSpec(memory_space=pltpu.VMEM...]
    all_to_all x1, waiting for transfers between devices: 18.4 us -> 14.2 us  [exchange(): return lax.all_to_all(pieces, axis, split_axis=0, concat_axis=0, tiled=True)]
    pallas_call x1, Pallas kernels: 3.93 us -> 0.7 us  [encode(): pl.pallas_call(encode_kernel, in_specs=[pl.BlockSpec(memory_space=pltpu.V...]
  transfers between devices with their start and end apart: 19 -> 19, of which waited for: 9 -> 11; matrix products, arithmetic and copies ran while one was open for 7% -> 8% of each run, Pallas kernels for 6% -> 3%
where the time goes in v4:
time: 129 us; the launch traced here: 126 us
  waiting for transfers between devices  42.1 us (33%)
  starting transfers between devices  41.6 us (32%)
  local copies, waits for them, and re-layouts  14.6 us (11%)
  blocking collectives  12 us (9%)
  other arithmetic  8.01 us (6%)
  Pallas kernels  4.79 us (4%)
  matrix products  2.1 us (2%)
    ppermute x15, waiting for transfers between devices, stepped(): return lax.ppermute(array, ('core', axis), pairs)  23.3 us
    ppermute x15, starting transfers between devices, stepped(): return lax.ppermute(array, ('core', axis), pairs)  21.6 us
    all_to_all x1, waiting for transfers between devices, exchange(): return lax.all_to_all(pieces, axis, split_axis=0, concat_axis=0, tiled=True)  14.2 us
    all_to_all x1, blocking collectives, exchange(): return lax.all_to_all(pieces, axis, split_axis=0, concat_axis=0, tiled=True)  12 us
    unnamed x23, local copies, waits for them, and re-layouts  11 us
    ppermute x1, starting transfers between devices, body(): recon = lax.ppermute(summed, ('zh', 'x'), swap)  7.85 us
    all_to_all x1, starting transfers between devices, exchange(): return lax.all_to_all(pieces, axis, split_axis=0, concat_axis=0, tiled=True)  7.45 us
    ppermute x2, starting transfers between devices, passed_on(): lax.ppermute(array, axis, [(index, (index + step) % count) for index in r...  4.68 us
  transfers between devices with their start and end apart: 19, of which 11 were waited for; matrix products, arithmetic and copies ran while one was open for 8% of the time, Pallas kernels for 3%

profile of v4, /device:TPU:4, one launch (start us, length us, event | category | flops | bytes accessed | tf_op | source)
XLA Modules:
  0.0 126.2 jit_solution(18068888537411972613)
XLA Ops:
  1.5 12.0 %all_to_all.10 = bf16[4,3,36,128]{3,2,1,0:T(8,128)(2,1)S(1)} all-to-all(bf16[4,3,36,128]{3,2,1,0:T(8,128)(2,1)S(1)} %broadcast_in_dim.6), channel_id=1, replica_groups=mesh['zh'=2,'core'=2,'x'=4,'y'=4,'zl'=4] {'zl'}, dimensions={0} | all-to-all | bytes 221184 | tf_op jit(solution)/shard_map/all_to_all | solution.py:16
  15.1 7.5 %all-to-all-start.1 = ((bf16[16,3,144,128]{3,2,1,0:T(8,128)(2,1)}), bf16[16,3,144,128]{3,2,1,0:T(8,128)(2,1)S(1)}, u32[]{:S(2)}, u32[]{:S(2)}) async-start(bf16[16,3,144,128]{3,2,1,0:T(8,128)(2,1)} %broadcast_in_dim.7), calls=%async_computation.1 | async-start | bytes 3538944 | tf_op jit(solution)/shard_map/all_to_all | solution.py:16
  22.5 2.0 %copy-done.3 = bf16[3,2304,256]{2,1,0:T(8,128)(2,1)S(1)} copy-done((bf16[3,2304,256]{2,1,0:T(8,128)(2,1)S(1)}, bf16[3,2304,256]{2,1,0:T(8,128)(2,1)}, u32[]{:S(2)}) %copy-start.3) | copy-done | bytes 3538968
  25.0 1.7 %copy-done = bf16[3,2304,256]{2,1,0:T(8,128)(2,1)} copy-done((bf16[3,2304,256]{2,1,0:T(8,128)(2,1)}, bf16[3,2304,256]{2,1,0:T(8,128)(2,1)S(1)}, u32[]{:S(2)}) %copy-start) | copy-done | bytes 3538968
  28.4 2.1 %pad_maximum_fusion = bf16[2,6,576,256]{3,2,0,1:T(8,128)(2,1)} fusion(bf16[1,6,576,256]{3,2,0,1:T(8,128)(2,1)S(1)} %get-tuple-element.13, bf16[1,6,576,256]{3,2,0,1:T(8,128)(2,1)S(1)} %get-tuple-element.12), kind=kLoop, calls=%fused_computation | loop fusion | flops 1769472 | bytes 7077888 | tf_op jit(solution)/shard_map/stack | solution.py:140
  30.6 14.2 %all-to-all-done.1.features = bf16[16,3,144,128]{3,2,1,0:T(8,128)(2,1)S(1)} async-done(((bf16[16,3,144,128]{3,2,1,0:T(8,128)(2,1)}), bf16[16,3,144,128]{3,2,1,0:T(8,128)(2,1)S(1)}, u32[]{:S(2)}, u32[]{:S(2)}) %all-to-all-start.1) | async-done | bytes 1769504 | tf_op jit(solution)/shard_map/all_to_all | solution.py:16
  44.8 2.0 %copy-done.1 = bf16[3,2304,256]{2,1,0:T(8,128)(2,1)S(1)} copy-done((bf16[3,2304,256]{2,1,0:T(8,128)(2,1)S(1)}, bf16[3,2304,256]{2,1,0:T(8,128)(2,1)}, u32[]{:S(2)}) %copy-start.1) | copy-done | bytes 3538968
  47.5 4.6 %collective-permute-start.1 = (bf16[3,128,256]{2,1,0:T(8,128)(2,1)S(1)}, bf16[3,128,256]{2,1,0:T(8,128)(2,1)S(1)}, u32[]{:S(2)}, u32[]{:S(2)}) collective-permute-start(bf16[3,128,256]{2,1,0:T(8,128)(2,1)S(1)} %encode.1), channel_id=1, source_target_pairs={{0,128},{128,0},{1,129},{129,1},{2,130},{130,2},{3,131},{131,3},{4... | collective-permute-start | bytes 589832 | tf_op jit(solution)/shard_map/ppermute | solution.py:33
  52.1 2.1 %copy-done.2 = bf16[3,2304,2,144]{1,3,2,0:T(8,128)(2,1)S(1)} copy-done((bf16[3,2304,2,144]{1,3,2,0:T(8,128)(2,1)S(1)}, bf16[3,2304,2,144]{1,3,2,0:T(8,128)(2,1)}, u32[]{:S(2)}) %copy-start.2) | copy-done | bytes 3981336
  55.8 3.7 %mlp.1 = bf16[3,16,144,128]{3,2,1,0:T(8,128)(2,1)S(1)} custom-call(bf16[16,3,144,128]{3,2,1,0:T(8,128)(2,1)S(1)} %all-to-all-done.1.features, bf16[3,2,144,2304]{3,2,1,0:T(8,128)(2,1)S(1)} %bitcast.133, bf16[3,144,2304]{2,1,0:T(8,128)(2,1)S(1)} %copy-done.4), custom_call_target="tpu_custom_call" | custom-call | flops 764411904 | bytes 9510912 | tf_op jit(solution)/shard_map/mlp/pallas_call | solution.py:117
  68.0 2.5 %collective-permute-start.4 = (bf16[6,4,72,128]{3,2,0,1:T(8,128)(2,1)S(1)}, bf16[6,4,72,128]{3,2,0,1:T(8,128)(2,1)S(1)}, u32[]{:S(2)}, u32[]{:S(2)}) collective-permute-start(bf16[6,4,72,128]{3,2,0,1:T(8,128)(2,1)S(1)} %bitcast.143), channel_id=1, source_target_pairs={{0,32},{16,48},{32,0},{48,16},{64,96},{80,112},{96,64},{112,80},{1... | collective-permute-start | bytes 1327112 | tf_op jit(solution)/shard_map/ppermute | solution.py:42
  71.8 6.8 %collective-permute-done.10 = bf16[6,4,72,128]{3,2,0,1:T(8,128)(2,1)} collective-permute-done((bf16[6,4,72,128]{3,2,0,1:T(8,128)(2,1)}, bf16[6,4,72,128]{3,2,0,1:T(8,128)(2,1)}, u32[]{:S(2)}, u32[]{:S(2)}) %collective-permute-start.10) | collective-permute-done | bytes 442400 | tf_op jit(solution)/shard_map/ppermute | solution.py:42
  78.6 1.9 %collective-permute-start.2 = (bf16[6,4,72,128]{3,2,0,1:T(8,128)(2,1)S(1)}, bf16[6,4,72,128]{3,2,0,1:T(8,128)(2,1)}, u32[]{:S(2)}, u32[]{:S(2)}) collective-permute-start(bf16[6,4,72,128]{3,2,0,1:T(8,128)(2,1)S(1)} %bitcast.142), channel_id=1, source_target_pairs={{0,16},{16,32},{32,48},{48,0},{64,112},{80,64},{96,80},{112,96},{1... | collective-permute-start | bytes 1327112 | tf_op jit(solution)/shard_map/ppermute | solution.py:42
  80.5 1.9 %collective-permute-done.9 = bf16[6,4,72,128]{3,2,0,1:T(8,128)(2,1)} collective-permute-done((bf16[6,4,72,128]{3,2,0,1:T(8,128)(2,1)S(1)}, bf16[6,4,72,128]{3,2,0,1:T(8,128)(2,1)}, u32[]{:S(2)}, u32[]{:S(2)}) %collective-permute-start.9) | collective-permute-done | bytes 442400 | tf_op jit(solution)/shard_map/ppermute | solution.py:42
  84.8 2.6 %collective-permute-start.13 = (bf16[6,72,128]{2,1,0:T(8,128)(2,1)S(1)}, bf16[6,72,128]{2,1,0:T(8,128)(2,1)S(1)}, u32[]{:S(2)}, u32[]{:S(2)}) collective-permute-start(bf16[6,72,128]{2,1,0:T(8,128)(2,1)S(1)} %get-tuple-element.29), channel_id=1, source_target_pairs={{0,32},{16,48},{32,0},{48,16},{64,96},{80,112},{96,64},{112,80},{1... | collective-permute-start | bytes 331784 | tf_op jit(solution)/shard_map/ppermute | solution.py:42
  92.5 2.5 %collective-permute-start.6 = (bf16[6,72,128]{2,1,0:T(8,128)(2,1)S(1)}, bf16[6,72,128]{2,1,0:T(8,128)(2,1)S(1)}, u32[]{:S(2)}, u32[]{:S(2)}) collective-permute-start(bf16[6,72,128]{2,1,0:T(8,128)(2,1)S(1)} %get-tuple-element.27), channel_id=1, source_target_pairs={{0,12},{4,0},{8,4},{12,8},{64,68},{68,72},{72,76},{76,64},{1,13},{... | collective-permute-start | bytes 331784 | tf_op jit(solution)/shard_map/ppermute | solution.py:42
  95.1 3.2 %collective-permute-done.7 = bf16[6,72,128]{2,1,0:T(8,128)(2,1)S(1)} collective-permute-done((bf16[6,72,128]{2,1,0:T(8,128)(2,1)S(1)}, bf16[6,72,128]{2,1,0:T(8,128)(2,1)S(1)}, u32[]{:S(2)}, u32[]{:S(2)}) %collective-permute-start.7) | collective-permute-done | bytes 110624 | tf_op jit(solution)/shard_map/ppermute | solution.py:42
  99.1 1.8 %collective-permute-done.5 = bf16[6,72,128]{2,1,0:T(8,128)(2,1)S(1)} collective-permute-done((bf16[6,72,128]{2,1,0:T(8,128)(2,1)S(1)}, bf16[6,72,128]{2,1,0:T(8,128)(2,1)S(1)}, u32[]{:S(2)}, u32[]{:S(2)}) %collective-permute-start.5) | collective-permute-done | bytes 110624 | tf_op jit(solution)/shard_map/ppermute | solution.py:42
  101.1 1.7 %collective-permute-start.16 = (f32[6,36,128]{2,1,0:T(8,128)S(1)}, f32[6,36,128]{2,1,0:T(8,128)S(1)}, u32[]{:S(2)}, u32[]{:S(2)}) collective-permute-start(f32[6,36,128]{2,1,0:T(8,128)S(1)} %get-tuple-element.23), channel_id=1, source_target_pairs={{0,2},{1,3},{2,0},{3,1},{64,66},{65,67},{66,64},{67,65},{4,6},{5,7... | collective-permute-start | bytes 331784 | tf_op jit(solution)/shard_map/ppermute | solution.py:42
  102.9 2.8 %collective-permute-start.15 = (f32[6,36,128]{2,1,0:T(8,128)S(1)}, f32[6,36,128]{2,1,0:T(8,128)S(1)}, u32[]{:S(2)}, u32[]{:S(2)}) collective-permute-start(f32[6,36,128]{2,1,0:T(8,128)S(1)} %get-tuple-element.24), channel_id=1, source_target_pairs={{0,3},{1,0},{2,1},{3,2},{64,65},{65,66},{66,67},{67,64},{4,7},{5,4... | collective-permute-start | bytes 331784 | tf_op jit(solution)/shard_map/ppermute | solution.py:42
  105.6 4.3 %collective-permute-done.16 = f32[6,36,128]{2,1,0:T(8,128)S(1)} collective-permute-done((f32[6,36,128]{2,1,0:T(8,128)S(1)}, f32[6,36,128]{2,1,0:T(8,128)S(1)}, u32[]{:S(2)}, u32[]{:S(2)}) %collective-permute-start.16) | collective-permute-done | bytes 110624 | tf_op jit(solution)/shard_map/ppermute | solution.py:42
  109.9 2.5 %collective-permute-done.14 = f32[6,36,128]{2,1,0:T(8,128)S(1)} collective-permute-done((f32[6,36,128]{2,1,0:T(8,128)S(1)}, f32[6,36,128]{2,1,0:T(8,128)S(1)}, u32[]{:S(2)}, u32[]{:S(2)}) %collective-permute-start.14) | collective-permute-done | bytes 110624 | tf_op jit(solution)/shard_map/ppermute | solution.py:42
  112.5 7.8 %collective-permute-start.17 = (f32[3,36,128]{2,1,0:T(8,128)S(1)}, f32[3,36,128]{2,1,0:T(8,128)S(1)}, u32[]{:S(2)}, u32[]{:S(2)}) collective-permute-start(f32[3,36,128]{2,1,0:T(8,128)S(1)} %slice.61), channel_id=1, source_target_pairs={{0,0},{16,16},{32,128},{48,144},{128,32},{144,48},{160,160},{176,1... | collective-permute-start | bytes 165896 | tf_op jit(solution)/shard_map/ppermute | solution.py:171
  120.3 4.6 %collective-permute-done.17 = f32[3,36,128]{2,1,0:T(8,128)S(1)} collective-permute-done((f32[3,36,128]{2,1,0:T(8,128)S(1)}, f32[3,36,128]{2,1,0:T(8,128)S(1)}, u32[]{:S(2)}, u32[]{:S(2)}) %collective-permute-start.17) | collective-permute-done | bytes 55328 | tf_op jit(solution)/shard_map/ppermute | solution.py:171
  (70 shorter events, 26.4 us)
Async XLA Ops:
  0.6 26.1 %collective-permute-start = (bf16[6,576,256]{2,1,0:T(8,128)(2,1)}, bf16[6,576,256]{2,1,0:T(8,128)(2,1)}, u32[]{:S(2)}, u32[]{:S(2)}) collective-permute-start(bf16[6,576,256]{2,1,0:T(8,128)(2,1)} %bitcast.137), channel_id=1, source_target_pairs={{0,64},{64,0},{1,65},{65,1},{2,66},{66,2},{3,67},{67,3},{4,68},{68... | collective-permute-start | bytes 5308424 | tf_op jit(solution)/shard_map/ppermute | solution.py:33
  15.1 29.7 %all-to-all-start.1 = ((bf16[16,3,144,128]{3,2,1,0:T(8,128)(2,1)}), bf16[16,3,144,128]{3,2,1,0:T(8,128)(2,1)S(1)}, u32[]{:S(2)}, u32[]{:S(2)}) async-start(bf16[16,3,144,128]{3,2,1,0:T(8,128)(2,1)} %broadcast_in_dim.7), calls=%async_computation.1 | async-start | bytes 3538944 | tf_op jit(solution)/shard_map/all_to_all | solution.py:16
  24.5 2.2 %copy-start.7 = (bf16[6,256,576]{1,2,0:T(8,128)(2,1)S(1)}, bf16[6,256,576]{1,2,0:T(8,128)(2,1)}, u32[]{:S(2)}) copy-start(bf16[6,256,576]{1,2,0:T(8,128)(2,1)} %param.11) | copy-start | bytes 5308420
  28.4 16.4 %copy-start.5 = (f32[3,256]{1,0:T(4,128)S(1)}, f32[3,256]{1,0:T(4,128)}, u32[]{:S(2)}) copy-start(f32[3,256]{1,0:T(4,128)} %bias.1) | copy-start | bytes 9220
  44.8 2.0 %copy-start.1 = (bf16[3,2304,256]{2,1,0:T(8,128)(2,1)S(1)}, bf16[3,2304,256]{2,1,0:T(8,128)(2,1)}, u32[]{:S(2)}) copy-start(bf16[3,2304,256]{2,1,0:T(8,128)(2,1)} %copy-done) | copy-start | bytes 10616836
  47.5 11.9 %collective-permute-start.1 = (bf16[3,128,256]{2,1,0:T(8,128)(2,1)S(1)}, bf16[3,128,256]{2,1,0:T(8,128)(2,1)S(1)}, u32[]{:S(2)}, u32[]{:S(2)}) collective-permute-start(bf16[3,128,256]{2,1,0:T(8,128)(2,1)S(1)} %encode.1), channel_id=1, source_target_pairs={{0,128},{128,0},{1,129},{129,1},{2,130},{130,2},{3,131},{131,3},{4... | collective-permute-start | bytes 589832 | tf_op jit(solution)/shard_map/ppermute | solution.py:33
  52.1 2.1 %copy-start.2 = (bf16[3,2304,2,144]{1,3,2,0:T(8,128)(2,1)S(1)}, bf16[3,2304,2,144]{1,3,2,0:T(8,128)(2,1)}, u32[]{:S(2)}) copy-start(bf16[3,2304,2,144]{1,3,2,0:T(8,128)(2,1)} %param.7) | copy-start | bytes 11943940
  55.8 3.7 %copy-start.6 = (bf16[2,6,576,256]{3,2,0,1:T(8,128)(2,1)S(1)}, bf16[2,6,576,256]{3,2,0,1:T(8,128)(2,1)}, u32[]{:S(2)}) copy-start(bf16[2,6,576,256]{3,2,0,1:T(8,128)(2,1)} %pad_maximum_fusion) | copy-start | bytes 10616836
  63.9 14.7 %collective-permute-start.10 = (bf16[6,4,72,128]{3,2,0,1:T(8,128)(2,1)}, bf16[6,4,72,128]{3,2,0,1:T(8,128)(2,1)}, u32[]{:S(2)}, u32[]{:S(2)}) collective-permute-start(bf16[6,4,72,128]{3,2,0,1:T(8,128)(2,1)} %bitcast.126), channel_id=1, source_target_pairs={{0,8},{4,12},{8,0},{12,4},{64,72},{68,76},{72,64},{76,68},{1,9},{5... | collective-permute-start | bytes 1327112 | tf_op jit(solution)/shard_map/ppermute | solution.py:42
  65.5 16.8 %collective-permute-start.9 = (bf16[6,4,72,128]{3,2,0,1:T(8,128)(2,1)S(1)}, bf16[6,4,72,128]{3,2,0,1:T(8,128)(2,1)}, u32[]{:S(2)}, u32[]{:S(2)}) collective-permute-start(bf16[6,4,72,128]{3,2,0,1:T(8,128)(2,1)S(1)} %bitcast.139), channel_id=1, source_target_pairs={{0,12},{4,0},{8,4},{12,8},{64,68},{68,72},{72,76},{76,64},{1,13},{... | collective-permute-start | bytes 1327112 | tf_op jit(solution)/shard_map/ppermute | solution.py:42
  67.3 16.0 %collective-permute-start.8 = (bf16[6,4,72,128]{3,2,0,1:T(8,128)(2,1)S(1)}, bf16[6,4,72,128]{3,2,0,1:T(8,128)(2,1)}, u32[]{:S(2)}, u32[]{:S(2)}) collective-permute-start(bf16[6,4,72,128]{3,2,0,1:T(8,128)(2,1)S(1)} %bitcast.140), channel_id=1, source_target_pairs={{0,4},{4,8},{8,12},{12,0},{64,76},{68,64},{72,68},{76,72},{1,5},{5... | collective-permute-start | bytes 1327112 | tf_op jit(solution)/shard_map/ppermute | solution.py:42
  68.0 20.3 %collective-permute-start.4 = (bf16[6,4,72,128]{3,2,0,1:T(8,128)(2,1)S(1)}, bf16[6,4,72,128]{3,2,0,1:T(8,128)(2,1)S(1)}, u32[]{:S(2)}, u32[]{:S(2)}) collective-permute-start(bf16[6,4,72,128]{3,2,0,1:T(8,128)(2,1)S(1)} %bitcast.143), channel_id=1, source_target_pairs={{0,32},{16,48},{32,0},{48,16},{64,96},{80,112},{96,64},{112,80},{1... | collective-permute-start | bytes 1327112 | tf_op jit(solution)/shard_map/ppermute | solution.py:42
  70.5 20.0 %collective-permute-start.3 = (bf16[6,4,72,128]{3,2,0,1:T(8,128)(2,1)S(1)}, bf16[6,4,72,128]{3,2,0,1:T(8,128)(2,1)}, u32[]{:S(2)}, u32[]{:S(2)}) collective-permute-start(bf16[6,4,72,128]{3,2,0,1:T(8,128)(2,1)S(1)} %bitcast.141), channel_id=1, source_target_pairs={{0,48},{16,0},{32,16},{48,32},{64,80},{80,96},{96,112},{112,64},{1... | collective-permute-start | bytes 1327112 | tf_op jit(solution)/shard_map/ppermute | solution.py:42
  78.6 11.9 %collective-permute-start.2 = (bf16[6,4,72,128]{3,2,0,1:T(8,128)(2,1)S(1)}, bf16[6,4,72,128]{3,2,0,1:T(8,128)(2,1)}, u32[]{:S(2)}, u32[]{:S(2)}) collective-permute-start(bf16[6,4,72,128]{3,2,0,1:T(8,128)(2,1)S(1)} %bitcast.142), channel_id=1, source_target_pairs={{0,16},{16,32},{32,48},{48,0},{64,112},{80,64},{96,80},{112,96},{1... | collective-permute-start | bytes 1327112 | tf_op jit(solution)/shard_map/ppermute | solution.py:42
  84.8 10.1 %collective-permute-start.13 = (bf16[6,72,128]{2,1,0:T(8,128)(2,1)S(1)}, bf16[6,72,128]{2,1,0:T(8,128)(2,1)S(1)}, u32[]{:S(2)}, u32[]{:S(2)}) collective-permute-start(bf16[6,72,128]{2,1,0:T(8,128)(2,1)S(1)} %get-tuple-element.29), channel_id=1, source_target_pairs={{0,32},{16,48},{32,0},{48,16},{64,96},{80,112},{96,64},{112,80},{1... | collective-permute-start | bytes 331784 | tf_op jit(solution)/shard_map/ppermute | solution.py:42
  87.4 7.6 %collective-permute-start.12 = (bf16[6,72,128]{2,1,0:T(8,128)(2,1)S(1)}, bf16[6,72,128]{2,1,0:T(8,128)(2,1)S(1)}, u32[]{:S(2)}, u32[]{:S(2)}) collective-permute-start(bf16[6,72,128]{2,1,0:T(8,128)(2,1)S(1)} %get-tuple-element.30), channel_id=1, source_target_pairs={{0,48},{16,0},{32,16},{48,32},{64,80},{80,96},{96,112},{112,64},{1... | collective-permute-start | bytes 331784 | tf_op jit(solution)/shard_map/ppermute | solution.py:42
  88.3 6.7 %collective-permute-start.11 = (bf16[6,72,128]{2,1,0:T(8,128)(2,1)S(1)}, bf16[6,72,128]{2,1,0:T(8,128)(2,1)S(1)}, u32[]{:S(2)}, u32[]{:S(2)}) collective-permute-start(bf16[6,72,128]{2,1,0:T(8,128)(2,1)S(1)} %get-tuple-element.28), channel_id=1, source_target_pairs={{0,16},{16,32},{32,48},{48,0},{64,112},{80,64},{96,80},{112,96},{1... | collective-permute-start | bytes 331784 | tf_op jit(solution)/shard_map/ppermute | solution.py:42
  91.9 6.3 %collective-permute-start.7 = (bf16[6,72,128]{2,1,0:T(8,128)(2,1)S(1)}, bf16[6,72,128]{2,1,0:T(8,128)(2,1)S(1)}, u32[]{:S(2)}, u32[]{:S(2)}) collective-permute-start(bf16[6,72,128]{2,1,0:T(8,128)(2,1)S(1)} %get-tuple-element.26), channel_id=1, source_target_pairs={{0,8},{4,12},{8,0},{12,4},{64,72},{68,76},{72,64},{76,68},{1,9},{5... | collective-permute-start | bytes 331784 | tf_op jit(solution)/shard_map/ppermute | solution.py:42
  92.5 6.6 %collective-permute-start.6 = (bf16[6,72,128]{2,1,0:T(8,128)(2,1)S(1)}, bf16[6,72,128]{2,1,0:T(8,128)(2,1)S(1)}, u32[]{:S(2)}, u32[]{:S(2)}) collective-permute-start(bf16[6,72,128]{2,1,0:T(8,128)(2,1)S(1)} %get-tuple-element.27), channel_id=1, source_target_pairs={{0,12},{4,0},{8,4},{12,8},{64,68},{68,72},{72,76},{76,64},{1,13},{... | collective-permute-start | bytes 331784 | tf_op jit(solution)/shard_map/ppermute | solution.py:42
  95.0 6.0 %collective-permute-start.5 = (bf16[6,72,128]{2,1,0:T(8,128)(2,1)S(1)}, bf16[6,72,128]{2,1,0:T(8,128)(2,1)S(1)}, u32[]{:S(2)}, u32[]{:S(2)}) collective-permute-start(bf16[6,72,128]{2,1,0:T(8,128)(2,1)S(1)} %get-tuple-element.25), channel_id=1, source_target_pairs={{0,4},{4,8},{8,12},{12,0},{64,76},{68,64},{72,68},{76,72},{1,5},{5... | collective-permute-start | bytes 331784 | tf_op jit(solution)/shard_map/ppermute | solution.py:42
  101.1 8.8 %collective-permute-start.16 = (f32[6,36,128]{2,1,0:T(8,128)S(1)}, f32[6,36,128]{2,1,0:T(8,128)S(1)}, u32[]{:S(2)}, u32[]{:S(2)}) collective-permute-start(f32[6,36,128]{2,1,0:T(8,128)S(1)} %get-tuple-element.23), channel_id=1, source_target_pairs={{0,2},{1,3},{2,0},{3,1},{64,66},{65,67},{66,64},{67,65},{4,6},{5,7... | collective-permute-start | bytes 331784 | tf_op jit(solution)/shard_map/ppermute | solution.py:42
  102.9 7.0 %collective-permute-start.15 = (f32[6,36,128]{2,1,0:T(8,128)S(1)}, f32[6,36,128]{2,1,0:T(8,128)S(1)}, u32[]{:S(2)}, u32[]{:S(2)}) collective-permute-start(f32[6,36,128]{2,1,0:T(8,128)S(1)} %get-tuple-element.24), channel_id=1, source_target_pairs={{0,3},{1,0},{2,1},{3,2},{64,65},{65,66},{66,67},{67,64},{4,7},{5,4... | collective-permute-start | bytes 331784 | tf_op jit(solution)/shard_map/ppermute | solution.py:42
  105.6 6.8 %collective-permute-start.14 = (f32[6,36,128]{2,1,0:T(8,128)S(1)}, f32[6,36,128]{2,1,0:T(8,128)S(1)}, u32[]{:S(2)}, u32[]{:S(2)}) collective-permute-start(f32[6,36,128]{2,1,0:T(8,128)S(1)} %get-tuple-element.22), channel_id=1, source_target_pairs={{0,1},{1,2},{2,3},{3,0},{64,67},{65,64},{66,65},{67,66},{4,5},{5,6... | collective-permute-start | bytes 331784 | tf_op jit(solution)/shard_map/ppermute | solution.py:42
  112.5 12.4 %collective-permute-start.17 = (f32[3,36,128]{2,1,0:T(8,128)S(1)}, f32[3,36,128]{2,1,0:T(8,128)S(1)}, u32[]{:S(2)}, u32[]{:S(2)}) collective-permute-start(f32[3,36,128]{2,1,0:T(8,128)S(1)} %slice.61), channel_id=1, source_target_pairs={{0,0},{16,16},{32,128},{48,144},{128,32},{144,48},{160,160},{176,1... | collective-permute-start | bytes 165896 | tf_op jit(solution)/shard_map/ppermute | solution.py:171
  (3 other events, 5.3 us)
